TPU v7x, 512 devices: a whole 4x8x8 slice. The times are simulated.
512 devices in a mesh: seq: 32 (over x, z), head: 16 (over y, core).
Axes of the slice: x: 4, y: 8, z: 8, core: 2. Of those that a mesh axis runs over, the one named last changes fastest.
Arguments:
- queries: bfloat16 [32768, 2048], P('seq', 'head'), may hold values from -6 to 6
- key_rows: bfloat16 [32768, 2048], P('seq', 'head'), may hold values from -6 to 6
- value_rows: bfloat16 [32768, 4096], P('seq', 'head'), may hold values from -6 to 6
- out_gate: bfloat16 [32768, 4096], P('seq', 'head'), may hold values from -6 to 6
- write_rate: float32 [32, 32768], P('head', 'seq'), may hold values from 0.0009765625 to 1
- log_gate: float32 [32, 32768], P('head', 'seq'), may hold values from -1 to 0, as said below
- doc_start: int32 [32768], P('seq'), may hold values 0 or 1
- norm_gain: float32 [128], replicated, may hold values from 0.1 to 1.9
- out_weight: bfloat16 [4096, 2048], P('head'), may hold values from -0.125 to 0.125
Outputs:
- mixed: bfloat16 [32768, 2048], P('seq', 'head')
Inputs may be any that keep to these rules, and one draw needn't show every extreme that they name: `log_gate`: log of the per-token decay factor of each value head's state.
All inputs are finite; a program needn't handle non-finite values. No bound on the sum of `doc_start` on one device may be relied on, other than what follows from the above.
Results may differ from a plain program's by a relative error of at most 0.027.
Values may be sent and summed in bfloat16 or wider, within the bound.
A program may use at most 128 MiB of HBM per device.

v0:
```python
import jax
import jax.numpy as jnp
from jax import lax
from jax.sharding import PartitionSpec as P

DK = 128
DV = 128
SPAN = 64


highest = lax.Precision.HIGHEST


def shifted(block, axis, distance):
    devices = range(lax.axis_size(axis))
    route = [(i - distance, i) for i in devices if i - distance in devices]
    return lax.ppermute(block, axis, route)


def unit_rows(values):
    return values * lax.rsqrt(jnp.sum(values * values, axis=-1, keepdims=True) + 1e-06)


def block_parts(queries, keys, values, rates, logs, starts):
    cumlog = jnp.cumsum(logs, axis=-1)
    resets = jnp.cumsum(starts, axis=-1)
    token_positions = jnp.arange(SPAN)
    lower_tri = token_positions[:, None] >= token_positions[None, :]
    same_doc = (resets[..., :, None] == resets[..., None, :]) & lower_tri
    log_gap = cumlog[..., :, None] - cumlog[..., None, :]
    decays = jnp.where(same_doc, jnp.exp(jnp.where(same_doc, log_gap, 0.0)), 0.0)
    last_log = cumlog[..., -1:]
    head_keep = jnp.exp(cumlog) * (resets == 0.0)
    tail_keep = jnp.exp(last_log - cumlog) * (resets == resets[..., -1:])
    whole_keep = jnp.exp(cumlog[..., -1]) * (resets[..., -1] == 0.0)
    identity = jnp.eye(SPAN, dtype=jnp.float32)
    key_inner = jnp.einsum("...ik,...jk->...ij", keys, keys, precision=highest)
    coupling = rates[..., :, None] * key_inner * decays * (1.0 - identity)
    inverse = identity - coupling
    powered = coupling
    extent = 1
    while 2 * extent < SPAN:
        powered = jnp.matmul(powered, powered, precision=highest)
        inverse = jnp.matmul(inverse, identity + powered, precision=highest)
        extent = extent * 2
    erase_keys = jnp.matmul(inverse, (rates * head_keep)[..., None] * keys, precision=highest)
    write_vals = jnp.matmul(inverse, rates[..., None] * values, precision=highest)
    scores = jnp.einsum("...ik,...jk->...ij", queries, keys, precision=highest) * decays
    return (queries, keys, erase_keys, write_vals, scores, head_keep, tail_keep, whole_keep)


def state_terms(parts, states):
    queries, keys, erase_keys, write_vals, scores, head_keep, tail_keep, whole_keep = parts
    seen = jnp.einsum("...ck,...vk->...cv", queries, states, precision=highest)
    erased = jnp.einsum("...ck,...vk->...cv", erase_keys, states, precision=highest)
    return (head_keep[..., None] * seen - jnp.matmul(scores, erased, precision=highest), erased)


def block_step(parts, state_now):
    queries, keys, erase_keys, write_vals, scores, head_keep, tail_keep, whole_keep = parts
    terms, erased = state_terms(parts, state_now)
    output = terms + jnp.matmul(scores, write_vals, precision=highest)
    fresh_vals = write_vals - erased
    state_next = whole_keep[..., None, None] * state_now + jnp.einsum(
        "...cv,...ck->...vk", tail_keep[..., None] * fresh_vals, keys, precision=highest
    )
    return (output, state_next)


def block_transition(parts):
    queries, keys, erase_keys, write_vals, scores, head_keep, tail_keep, whole_keep = parts
    eye_keys = jnp.eye(DK, dtype=jnp.float32)
    moves = whole_keep[..., None, None] * eye_keys - jnp.einsum(
        "...ck,...cj->...kj", erase_keys, tail_keep[..., None] * keys, precision=highest
    )
    carried = jnp.einsum(
        "...cv,...ck->...vk", tail_keep[..., None] * write_vals, keys, precision=highest
    )
    return (moves, carried)


def blocks_first(array_in):
    return jnp.moveaxis(array_in, 1, 0)


def local(
    queries, key_rows, value_rows, out_gate, write_rate, log_gate, doc_start, norm_gain, out_weight
):
    tokens_here = queries.shape[0]
    heads_here = value_rows.shape[1] // DV
    keys_here = key_rows.shape[1] // DK
    per_key = heads_here // keys_here
    blocks = tokens_here // SPAN

    def by_head(values, width):
        spread = values.reshape(blocks, SPAN, heads_here, width)
        return jnp.transpose(spread, (2, 0, 1, 3))

    query_unit = unit_rows(queries.astype(jnp.float32).reshape(tokens_here, keys_here, DK))
    key_unit = unit_rows(key_rows.astype(jnp.float32).reshape(tokens_here, keys_here, DK))
    query_heads = by_head(jnp.repeat(query_unit, per_key, axis=1), DK)
    key_heads = by_head(jnp.repeat(key_unit, per_key, axis=1), DK)
    value_heads = by_head(value_rows.astype(jnp.float32).reshape(tokens_here, heads_here, DV), DV)
    rates = write_rate.reshape(heads_here, blocks, SPAN)
    logs = log_gate.reshape(heads_here, blocks, SPAN)
    starts = jnp.broadcast_to(
        doc_start.astype(jnp.float32).reshape(1, blocks, SPAN), (heads_here, blocks, SPAN)
    )
    parts = block_parts(query_heads, key_heads, value_heads, rates, logs, starts)
    moves, carried = block_transition(parts)
    eye_heads = jnp.broadcast_to(jnp.eye(DK, dtype=jnp.float32), (heads_here, DK, DK))
    empty = jnp.zeros((heads_here, DV, DK), jnp.float32)

    def fold_blocks(carry, pair):
        total_move, total_state = carry
        move_now, carried_now = pair
        next_move = jnp.matmul(total_move, move_now, precision=highest)
        next_state = jnp.matmul(total_state, move_now, precision=highest) + carried_now
        return ((next_move, next_state), carry)

    (shard_move, shard_state), (prefix_moves, prefix_states) = lax.scan(
        fold_blocks, (eye_heads, empty), (blocks_first(moves), blocks_first(carried))
    )

    def pass_state(round_index, start_state):
        shard_end = jnp.matmul(start_state, shard_move, precision=highest) + shard_state
        return shifted(shard_end.astype(jnp.bfloat16), "seq", 1).astype(shard_end.dtype)

    start_state = lax.fori_loop(0, lax.axis_size("seq") - 1, pass_state, empty)

    def advance(state_now, inputs_now):
        output, state_next = block_step(inputs_now, state_now)
        return (state_next, output)

    final_state, outputs = lax.scan(advance, start_state, jax.tree.map(blocks_first, parts))
    attended = blocks_first(outputs)
    attended = jnp.transpose(attended, (1, 2, 0, 3)).reshape(tokens_here, heads_here, DV)
    gate_vals = out_gate.astype(jnp.float32).reshape(tokens_here, heads_here, DV)
    scale_rows = lax.rsqrt(jnp.mean(attended * attended, axis=-1, keepdims=True) + 1e-06)
    normed = (attended * scale_rows * norm_gain * jax.nn.silu(gate_vals)).astype(jnp.bfloat16)
    normed = normed.reshape(tokens_here, heads_here * DV)
    summed = lax.psum_scatter(
        lax.dot_general(
            out_weight, normed, (((0,), (1,)), ((), ())), preferred_element_type=jnp.float32
        ).astype(jnp.bfloat16),
        "head",
        scatter_dimension=0,
        tiled=True,
    )
    return jnp.transpose(summed)


def solution(mesh):
    placed = (
        P("seq", "head"),
        P("seq", "head"),
        P("seq", "head"),
        P("seq", "head"),
        P("head", "seq"),
        P("head", "seq"),
        P("seq"),
        P(),
        P("head", None),
    )
    return jax.shard_map(
        local, mesh=mesh, in_specs=placed, out_specs=P("seq", "head"), check_vma=False
    )
```

profile of v0, /device:TPU:6, one launch (start us, length us, event | category | flops | bytes accessed | tf_op | source)
XLA Modules:
  0.0 572.3 jit_solution(17418361937246625916)
XLA Ops:
  13.7 2.0 fusion.43
  24.1 2.2 convolution_add_fusion.3
  26.3 2.3 fusion.55
  30.1 2.5 fusion.94
  33.9 2.2 fusion.53
  36.8 5.1 convolution_bitcast_fusion.2
  41.9 5.6 bitcast_subtract_fusion.1
  47.5 59.2 %while.37 = (s32[]{:T(128)}, f32[2,128,128]{1,2,0:T(8,128)S(1)}, f32[2,128,128]{1,2,0:T(8,128)S(1)}, f32[16,2,128,128]{3,2,0,1:T(8,128)}, f32[16,2,128,128]{3,2,0,1:T(8,128)}, /*index=5*/s32[]{:T(128)}, s32[]{:T(128)}) while((s32[]{:T(128)}, f32[2,128,128]{1,2,0:T(8,128)S(1)}, f32[2,128,128]{1,2,0:T(8,128)S(1)}, ...), condition=%wide.region_4.5_spmd.clone, body=%wide.region_3.4_spmd.clone.sunk | while | flops 100728832 | bytes 1967195 | solution.py:121
  108.3 3.6 fusion.41
  111.9 272.6 %while.38 = (s32[]{:T(128)}, f32[2,128,128]{2,1,0:T(8,128)S(1)}, f32[2,128,128]{2,1,0:T(8,128)S(1)}, f32[2,128,128]{2,1,0:T(8,128)S(1)}, s32[]{:T(128)}, /*index=5*/s32[]{:T(128)}) while((s32[]{:T(128)}, f32[2,128,128]{2,1,0:T(8,128)S(1)}, f32[2,128,128]{2,1,0:T(8,128)S(1)}, f32[2,128,128]{2,1,0:T(8,128)S(1)}, s32[]{:T(128)}, ...), condition=%wide.region_6.7_spmd.clone, body=%wide.region_5.6_spmd.clone.sunk | while | flops 50462720 | bytes 917623 | solution.py:129
  112.2 4.3 collective-permute-start
  116.5 9.2 %collective-permute-done = bf16[2,128,128]{2,1,0:T(8,128)(2,1)S(1)} collective-permute-done((bf16[2,128,128]{2,1,0:T(8,128)(2,1)S(1)}, bf16[2,128,128]{2,1,0:T(8,128)(2,1)S(1)}, u32[]{:S(2)}, u32[]{:S(2)}) %collective-permute-start) | collective-permute-done | bytes 65568 | tf_op jit(solution)/shard_map/while/body/eval_jaxpr/ppermute | solution.py:17
  127.9 6.3 %collective-permute-done = bf16[2,128,128]{2,1,0:T(8,128)(2,1)S(1)} collective-permute-done((bf16[2,128,128]{2,1,0:T(8,128)(2,1)S(1)}, bf16[2,128,128]{2,1,0:T(8,128)(2,1)S(1)}, u32[]{:S(2)}, u32[]{:S(2)}) %collective-permute-start) | collective-permute-done | bytes 65568 | tf_op jit(solution)/shard_map/while/body/eval_jaxpr/ppermute | solution.py:17
  136.5 6.3 %collective-permute-done = bf16[2,128,128]{2,1,0:T(8,128)(2,1)S(1)} collective-permute-done((bf16[2,128,128]{2,1,0:T(8,128)(2,1)S(1)}, bf16[2,128,128]{2,1,0:T(8,128)(2,1)S(1)}, u32[]{:S(2)}, u32[]{:S(2)}) %collective-permute-start) | collective-permute-done | bytes 65568 | tf_op jit(solution)/shard_map/while/body/eval_jaxpr/ppermute | solution.py:17
  145.1 6.3 %collective-permute-done = bf16[2,128,128]{2,1,0:T(8,128)(2,1)S(1)} collective-permute-done((bf16[2,128,128]{2,1,0:T(8,128)(2,1)S(1)}, bf16[2,128,128]{2,1,0:T(8,128)(2,1)S(1)}, u32[]{:S(2)}, u32[]{:S(2)}) %collective-permute-start) | collective-permute-done | bytes 65568 | tf_op jit(solution)/shard_map/while/body/eval_jaxpr/ppermute | solution.py:17
  153.6 6.3 %collective-permute-done = bf16[2,128,128]{2,1,0:T(8,128)(2,1)S(1)} collective-permute-done((bf16[2,128,128]{2,1,0:T(8,128)(2,1)S(1)}, bf16[2,128,128]{2,1,0:T(8,128)(2,1)S(1)}, u32[]{:S(2)}, u32[]{:S(2)}) %collective-permute-start) | collective-permute-done | bytes 65568 | tf_op jit(solution)/shard_map/while/body/eval_jaxpr/ppermute | solution.py:17
  162.2 6.3 %collective-permute-done = bf16[2,128,128]{2,1,0:T(8,128)(2,1)S(1)} collective-permute-done((bf16[2,128,128]{2,1,0:T(8,128)(2,1)S(1)}, bf16[2,128,128]{2,1,0:T(8,128)(2,1)S(1)}, u32[]{:S(2)}, u32[]{:S(2)}) %collective-permute-start) | collective-permute-done | bytes 65568 | tf_op jit(solution)/shard_map/while/body/eval_jaxpr/ppermute | solution.py:17
  168.9 1.9 collective-permute-start
  170.8 6.7 %collective-permute-done = bf16[2,128,128]{2,1,0:T(8,128)(2,1)S(1)} collective-permute-done((bf16[2,128,128]{2,1,0:T(8,128)(2,1)S(1)}, bf16[2,128,128]{2,1,0:T(8,128)(2,1)S(1)}, u32[]{:S(2)}, u32[]{:S(2)}) %collective-permute-start) | collective-permute-done | bytes 65568 | tf_op jit(solution)/shard_map/while/body/eval_jaxpr/ppermute | solution.py:17
  177.8 1.9 collective-permute-start
  179.8 6.3 %collective-permute-done = bf16[2,128,128]{2,1,0:T(8,128)(2,1)S(1)} collective-permute-done((bf16[2,128,128]{2,1,0:T(8,128)(2,1)S(1)}, bf16[2,128,128]{2,1,0:T(8,128)(2,1)S(1)}, u32[]{:S(2)}, u32[]{:S(2)}) %collective-permute-start) | collective-permute-done | bytes 65568 | tf_op jit(solution)/shard_map/while/body/eval_jaxpr/ppermute | solution.py:17
  188.3 6.3 %collective-permute-done = bf16[2,128,128]{2,1,0:T(8,128)(2,1)S(1)} collective-permute-done((bf16[2,128,128]{2,1,0:T(8,128)(2,1)S(1)}, bf16[2,128,128]{2,1,0:T(8,128)(2,1)S(1)}, u32[]{:S(2)}, u32[]{:S(2)}) %collective-permute-start) | collective-permute-done | bytes 65568 | tf_op jit(solution)/shard_map/while/body/eval_jaxpr/ppermute | solution.py:17
  196.9 6.3 %collective-permute-done = bf16[2,128,128]{2,1,0:T(8,128)(2,1)S(1)} collective-permute-done((bf16[2,128,128]{2,1,0:T(8,128)(2,1)S(1)}, bf16[2,128,128]{2,1,0:T(8,128)(2,1)S(1)}, u32[]{:S(2)}, u32[]{:S(2)}) %collective-permute-start) | collective-permute-done | bytes 65568 | tf_op jit(solution)/shard_map/while/body/eval_jaxpr/ppermute | solution.py:17
  205.5 6.3 %collective-permute-done = bf16[2,128,128]{2,1,0:T(8,128)(2,1)S(1)} collective-permute-done((bf16[2,128,128]{2,1,0:T(8,128)(2,1)S(1)}, bf16[2,128,128]{2,1,0:T(8,128)(2,1)S(1)}, u32[]{:S(2)}, u32[]{:S(2)}) %collective-permute-start) | collective-permute-done | bytes 65568 | tf_op jit(solution)/shard_map/while/body/eval_jaxpr/ppermute | solution.py:17
  214.1 6.3 %collective-permute-done = bf16[2,128,128]{2,1,0:T(8,128)(2,1)S(1)} collective-permute-done((bf16[2,128,128]{2,1,0:T(8,128)(2,1)S(1)}, bf16[2,128,128]{2,1,0:T(8,128)(2,1)S(1)}, u32[]{:S(2)}, u32[]{:S(2)}) %collective-permute-start) | collective-permute-done | bytes 65568 | tf_op jit(solution)/shard_map/while/body/eval_jaxpr/ppermute | solution.py:17
  222.7 6.6 %collective-permute-done = bf16[2,128,128]{2,1,0:T(8,128)(2,1)S(1)} collective-permute-done((bf16[2,128,128]{2,1,0:T(8,128)(2,1)S(1)}, bf16[2,128,128]{2,1,0:T(8,128)(2,1)S(1)}, u32[]{:S(2)}, u32[]{:S(2)}) %collective-permute-start) | collective-permute-done | bytes 65568 | tf_op jit(solution)/shard_map/while/body/eval_jaxpr/ppermute | solution.py:17
  231.5 6.3 %collective-permute-done = bf16[2,128,128]{2,1,0:T(8,128)(2,1)S(1)} collective-permute-done((bf16[2,128,128]{2,1,0:T(8,128)(2,1)S(1)}, bf16[2,128,128]{2,1,0:T(8,128)(2,1)S(1)}, u32[]{:S(2)}, u32[]{:S(2)}) %collective-permute-start) | collective-permute-done | bytes 65568 | tf_op jit(solution)/shard_map/while/body/eval_jaxpr/ppermute | solution.py:17
  240.1 6.3 %collective-permute-done = bf16[2,128,128]{2,1,0:T(8,128)(2,1)S(1)} collective-permute-done((bf16[2,128,128]{2,1,0:T(8,128)(2,1)S(1)}, bf16[2,128,128]{2,1,0:T(8,128)(2,1)S(1)}, u32[]{:S(2)}, u32[]{:S(2)}) %collective-permute-start) | collective-permute-done | bytes 65568 | tf_op jit(solution)/shard_map/while/body/eval_jaxpr/ppermute | solution.py:17
  248.7 6.3 %collective-permute-done = bf16[2,128,128]{2,1,0:T(8,128)(2,1)S(1)} collective-permute-done((bf16[2,128,128]{2,1,0:T(8,128)(2,1)S(1)}, bf16[2,128,128]{2,1,0:T(8,128)(2,1)S(1)}, u32[]{:S(2)}, u32[]{:S(2)}) %collective-permute-start) | collective-permute-done | bytes 65568 | tf_op jit(solution)/shard_map/while/body/eval_jaxpr/ppermute | solution.py:17
  257.3 6.3 %collective-permute-done = bf16[2,128,128]{2,1,0:T(8,128)(2,1)S(1)} collective-permute-done((bf16[2,128,128]{2,1,0:T(8,128)(2,1)S(1)}, bf16[2,128,128]{2,1,0:T(8,128)(2,1)S(1)}, u32[]{:S(2)}, u32[]{:S(2)}) %collective-permute-start) | collective-permute-done | bytes 65568 | tf_op jit(solution)/shard_map/while/body/eval_jaxpr/ppermute | solution.py:17
  265.9 6.3 %collective-permute-done = bf16[2,128,128]{2,1,0:T(8,128)(2,1)S(1)} collective-permute-done((bf16[2,128,128]{2,1,0:T(8,128)(2,1)S(1)}, bf16[2,128,128]{2,1,0:T(8,128)(2,1)S(1)}, u32[]{:S(2)}, u32[]{:S(2)}) %collective-permute-start) | collective-permute-done | bytes 65568 | tf_op jit(solution)/shard_map/while/body/eval_jaxpr/ppermute | solution.py:17
  274.4 6.3 %collective-permute-done = bf16[2,128,128]{2,1,0:T(8,128)(2,1)S(1)} collective-permute-done((bf16[2,128,128]{2,1,0:T(8,128)(2,1)S(1)}, bf16[2,128,128]{2,1,0:T(8,128)(2,1)S(1)}, u32[]{:S(2)}, u32[]{:S(2)}) %collective-permute-start) | collective-permute-done | bytes 65568 | tf_op jit(solution)/shard_map/while/body/eval_jaxpr/ppermute | solution.py:17
  283.0 6.8 %collective-permute-done = bf16[2,128,128]{2,1,0:T(8,128)(2,1)S(1)} collective-permute-done((bf16[2,128,128]{2,1,0:T(8,128)(2,1)S(1)}, bf16[2,128,128]{2,1,0:T(8,128)(2,1)S(1)}, u32[]{:S(2)}, u32[]{:S(2)}) %collective-permute-start) | collective-permute-done | bytes 65568 | tf_op jit(solution)/shard_map/while/body/eval_jaxpr/ppermute | solution.py:17
  292.1 6.3 %collective-permute-done = bf16[2,128,128]{2,1,0:T(8,128)(2,1)S(1)} collective-permute-done((bf16[2,128,128]{2,1,0:T(8,128)(2,1)S(1)}, bf16[2,128,128]{2,1,0:T(8,128)(2,1)S(1)}, u32[]{:S(2)}, u32[]{:S(2)}) %collective-permute-start) | collective-permute-done | bytes 65568 | tf_op jit(solution)/shard_map/while/body/eval_jaxpr/ppermute | solution.py:17
  300.7 6.3 %collective-permute-done = bf16[2,128,128]{2,1,0:T(8,128)(2,1)S(1)} collective-permute-done((bf16[2,128,128]{2,1,0:T(8,128)(2,1)S(1)}, bf16[2,128,128]{2,1,0:T(8,128)(2,1)S(1)}, u32[]{:S(2)}, u32[]{:S(2)}) %collective-permute-start) | collective-permute-done | bytes 65568 | tf_op jit(solution)/shard_map/while/body/eval_jaxpr/ppermute | solution.py:17
  309.3 6.3 %collective-permute-done = bf16[2,128,128]{2,1,0:T(8,128)(2,1)S(1)} collective-permute-done((bf16[2,128,128]{2,1,0:T(8,128)(2,1)S(1)}, bf16[2,128,128]{2,1,0:T(8,128)(2,1)S(1)}, u32[]{:S(2)}, u32[]{:S(2)}) %collective-permute-start) | collective-permute-done | bytes 65568 | tf_op jit(solution)/shard_map/while/body/eval_jaxpr/ppermute | solution.py:17
  317.8 6.3 %collective-permute-done = bf16[2,128,128]{2,1,0:T(8,128)(2,1)S(1)} collective-permute-done((bf16[2,128,128]{2,1,0:T(8,128)(2,1)S(1)}, bf16[2,128,128]{2,1,0:T(8,128)(2,1)S(1)}, u32[]{:S(2)}, u32[]{:S(2)}) %collective-permute-start) | collective-permute-done | bytes 65568 | tf_op jit(solution)/shard_map/while/body/eval_jaxpr/ppermute | solution.py:17
  326.4 6.3 %collective-permute-done = bf16[2,128,128]{2,1,0:T(8,128)(2,1)S(1)} collective-permute-done((bf16[2,128,128]{2,1,0:T(8,128)(2,1)S(1)}, bf16[2,128,128]{2,1,0:T(8,128)(2,1)S(1)}, u32[]{:S(2)}, u32[]{:S(2)}) %collective-permute-start) | collective-permute-done | bytes 65568 | tf_op jit(solution)/shard_map/while/body/eval_jaxpr/ppermute | solution.py:17
  335.0 6.5 %collective-permute-done = bf16[2,128,128]{2,1,0:T(8,128)(2,1)S(1)} collective-permute-done((bf16[2,128,128]{2,1,0:T(8,128)(2,1)S(1)}, bf16[2,128,128]{2,1,0:T(8,128)(2,1)S(1)}, u32[]{:S(2)}, u32[]{:S(2)}) %collective-permute-start) | collective-permute-done | bytes 65568 | tf_op jit(solution)/shard_map/while/body/eval_jaxpr/ppermute | solution.py:17
  343.7 6.4 %collective-permute-done = bf16[2,128,128]{2,1,0:T(8,128)(2,1)S(1)} collective-permute-done((bf16[2,128,128]{2,1,0:T(8,128)(2,1)S(1)}, bf16[2,128,128]{2,1,0:T(8,128)(2,1)S(1)}, u32[]{:S(2)}, u32[]{:S(2)}) %collective-permute-start) | collective-permute-done | bytes 65568 | tf_op jit(solution)/shard_map/while/body/eval_jaxpr/ppermute | solution.py:17
  352.4 6.3 %collective-permute-done = bf16[2,128,128]{2,1,0:T(8,128)(2,1)S(1)} collective-permute-done((bf16[2,128,128]{2,1,0:T(8,128)(2,1)S(1)}, bf16[2,128,128]{2,1,0:T(8,128)(2,1)S(1)}, u32[]{:S(2)}, u32[]{:S(2)}) %collective-permute-start) | collective-permute-done | bytes 65568 | tf_op jit(solution)/shard_map/while/body/eval_jaxpr/ppermute | solution.py:17
  361.0 6.3 %collective-permute-done = bf16[2,128,128]{2,1,0:T(8,128)(2,1)S(1)} collective-permute-done((bf16[2,128,128]{2,1,0:T(8,128)(2,1)S(1)}, bf16[2,128,128]{2,1,0:T(8,128)(2,1)S(1)}, u32[]{:S(2)}, u32[]{:S(2)}) %collective-permute-start) | collective-permute-done | bytes 65568 | tf_op jit(solution)/shard_map/while/body/eval_jaxpr/ppermute | solution.py:17
  369.6 6.3 %collective-permute-done = bf16[2,128,128]{2,1,0:T(8,128)(2,1)S(1)} collective-permute-done((bf16[2,128,128]{2,1,0:T(8,128)(2,1)S(1)}, bf16[2,128,128]{2,1,0:T(8,128)(2,1)S(1)}, u32[]{:S(2)}, u32[]{:S(2)}) %collective-permute-start) | collective-permute-done | bytes 65568 | tf_op jit(solution)/shard_map/while/body/eval_jaxpr/ppermute | solution.py:17
  378.2 6.3 %collective-permute-done = bf16[2,128,128]{2,1,0:T(8,128)(2,1)S(1)} collective-permute-done((bf16[2,128,128]{2,1,0:T(8,128)(2,1)S(1)}, bf16[2,128,128]{2,1,0:T(8,128)(2,1)S(1)}, u32[]{:S(2)}, u32[]{:S(2)}) %collective-permute-start) | collective-permute-done | bytes 65568 | tf_op jit(solution)/shard_map/while/body/eval_jaxpr/ppermute | solution.py:17
  386.8 101.8 %while.36 = (s32[]{:T(128)}, f32[2,128,128]{2,1,0:T(8,128)S(1)}, f32[16,2,64,128]{3,2,1,0:T(8,128)}, f32[16,2]{1,0:T(8,128)}, f32[16,2,64]{2,0,1:T(8,128)S(1)}, ...) while((s32[]{:T(128)}, f32[2,128,128]{2,1,0:T(8,128)S(1)}, ...), condition=%wide.region_9.10_spmd, body=%wide.region_8.9_spmd.sunk | while | flops 100810752 | bytes 1515665 | solution.py:135
  492.7 3.4 convert_bitcast_fusion
  496.1 6.4 %copy.91 = bf16[2048,1024]{1,0:T(8,128)(2,1)} copy(bf16[2048,1024]{0,1:T(8,128)(2,1)} %convert_bitcast_fusion) | data formatting | bytes 8388608
  502.5 61.1 %reduce-scatter.4.cloned.1.call-done = bf16[128,1024]{1,0:T(8,128)(2,1)} async-done(((bf16[2048,1024]{1,0:T(8,128)(2,1)}), bf16[128,1024]{1,0:T(8,128)(2,1)}) %reduce-scatter.4.cloned.1.call-update) | async-done | bytes 262160
  (379 shorter events, 250.3 us)
Async XLA Ops:
  6.5 486.2 %copy-start = (bf16[256,2048]{1,0:T(8,128)(2,1)S(1)}, bf16[256,2048]{1,0:T(8,128)(2,1)}, u32[]{:S(2)}) copy-start(bf16[256,2048]{1,0:T(8,128)(2,1)} %param.23) | copy-start | bytes 3145732
  6.5 557.1 %reduce-scatter.4.cloned.1.call-start = ((), (), s32[]{:S(2)}) async-start(), calls=%async_computation.1 | async-start | bytes 4456448
  6.6 9.1 %copy-start.13 = (pred[64,64]{1,0:T(8,128)(4,1)}, pred[64,64]{1,0:T(8,128)(4,1)S(1)}, u32[]{:S(2)}) copy-start(pred[64,64]{1,0:T(8,128)(4,1)S(1)} %iota_compare_fusion.1) | copy-start | bytes 12292
  11.5 5.4 copy-start.8
  12.4 4.4 copy-start.10
  12.4 4.4 copy-start.11
  26.3 2.3 copy-start.7
  28.6 1.5 copy-start.2
  30.1 2.5 copy-start.3
  32.6 1.2 copy-start.9
  33.8 2.3 copy-start.12
  36.8 5.1 copy-start.1
  47.5 59.5 %copy-start.6 = (bf16[1024,128]{1,0:T(8,128)(2,1)S(1)}, bf16[1024,128]{1,0:T(8,128)(2,1)}, u32[]{:S(2)}) copy-start(bf16[1024,128]{1,0:T(8,128)(2,1)} %param.15) | copy-start | bytes 786436
  107.4 0.9 copy-start.5
  112.2 13.5 %collective-permute-start = (bf16[2,128,128]{2,1,0:T(8,128)(2,1)S(1)}, bf16[2,128,128]{2,1,0:T(8,128)(2,1)S(1)}, u32[]{:S(2)}, u32[]{:S(2)}) collective-permute-start(bf16[2,128,128]{2,1,0:T(8,128)(2,1)S(1)} %fusion.160), channel_id=1, source_target_pairs={{0,16},{16,32},{32,48},{48,64},{64,80},{80,96},{96,112},{112,128},... | collective-permute-start | bytes 196616 | tf_op jit(solution)/shard_map/while/body/eval_jaxpr/ppermute | solution.py:17
  126.0 8.3 %collective-permute-start = (bf16[2,128,128]{2,1,0:T(8,128)(2,1)S(1)}, bf16[2,128,128]{2,1,0:T(8,128)(2,1)S(1)}, u32[]{:S(2)}, u32[]{:S(2)}) collective-permute-start(bf16[2,128,128]{2,1,0:T(8,128)(2,1)S(1)} %fusion.160), channel_id=1, source_target_pairs={{0,16},{16,32},{32,48},{48,64},{64,80},{80,96},{96,112},{112,128},... | collective-permute-start | bytes 196616 | tf_op jit(solution)/shard_map/while/body/eval_jaxpr/ppermute | solution.py:17
  134.5 8.3 %collective-permute-start = (bf16[2,128,128]{2,1,0:T(8,128)(2,1)S(1)}, bf16[2,128,128]{2,1,0:T(8,128)(2,1)S(1)}, u32[]{:S(2)}, u32[]{:S(2)}) collective-permute-start(bf16[2,128,128]{2,1,0:T(8,128)(2,1)S(1)} %fusion.160), channel_id=1, source_target_pairs={{0,16},{16,32},{32,48},{48,64},{64,80},{80,96},{96,112},{112,128},... | collective-permute-start | bytes 196616 | tf_op jit(solution)/shard_map/while/body/eval_jaxpr/ppermute | solution.py:17
  143.1 8.3 %collective-permute-start = (bf16[2,128,128]{2,1,0:T(8,128)(2,1)S(1)}, bf16[2,128,128]{2,1,0:T(8,128)(2,1)S(1)}, u32[]{:S(2)}, u32[]{:S(2)}) collective-permute-start(bf16[2,128,128]{2,1,0:T(8,128)(2,1)S(1)} %fusion.160), channel_id=1, source_target_pairs={{0,16},{16,32},{32,48},{48,64},{64,80},{80,96},{96,112},{112,128},... | collective-permute-start | bytes 196616 | tf_op jit(solution)/shard_map/while/body/eval_jaxpr/ppermute | solution.py:17
  151.7 8.3 %collective-permute-start = (bf16[2,128,128]{2,1,0:T(8,128)(2,1)S(1)}, bf16[2,128,128]{2,1,0:T(8,128)(2,1)S(1)}, u32[]{:S(2)}, u32[]{:S(2)}) collective-permute-start(bf16[2,128,128]{2,1,0:T(8,128)(2,1)S(1)} %fusion.160), channel_id=1, source_target_pairs={{0,16},{16,32},{32,48},{48,64},{64,80},{80,96},{96,112},{112,128},... | collective-permute-start | bytes 196616 | tf_op jit(solution)/shard_map/while/body/eval_jaxpr/ppermute | solution.py:17
  160.3 8.3 %collective-permute-start = (bf16[2,128,128]{2,1,0:T(8,128)(2,1)S(1)}, bf16[2,128,128]{2,1,0:T(8,128)(2,1)S(1)}, u32[]{:S(2)}, u32[]{:S(2)}) collective-permute-start(bf16[2,128,128]{2,1,0:T(8,128)(2,1)S(1)} %fusion.160), channel_id=1, source_target_pairs={{0,16},{16,32},{32,48},{48,64},{64,80},{80,96},{96,112},{112,128},... | collective-permute-start | bytes 196616 | tf_op jit(solution)/shard_map/while/body/eval_jaxpr/ppermute | solution.py:17
  168.9 8.6 %collective-permute-start = (bf16[2,128,128]{2,1,0:T(8,128)(2,1)S(1)}, bf16[2,128,128]{2,1,0:T(8,128)(2,1)S(1)}, u32[]{:S(2)}, u32[]{:S(2)}) collective-permute-start(bf16[2,128,128]{2,1,0:T(8,128)(2,1)S(1)} %fusion.160), channel_id=1, source_target_pairs={{0,16},{16,32},{32,48},{48,64},{64,80},{80,96},{96,112},{112,128},... | collective-permute-start | bytes 196616 | tf_op jit(solution)/shard_map/while/body/eval_jaxpr/ppermute | solution.py:17
  177.8 8.3 %collective-permute-start = (bf16[2,128,128]{2,1,0:T(8,128)(2,1)S(1)}, bf16[2,128,128]{2,1,0:T(8,128)(2,1)S(1)}, u32[]{:S(2)}, u32[]{:S(2)}) collective-permute-start(bf16[2,128,128]{2,1,0:T(8,128)(2,1)S(1)} %fusion.160), channel_id=1, source_target_pairs={{0,16},{16,32},{32,48},{48,64},{64,80},{80,96},{96,112},{112,128},... | collective-permute-start | bytes 196616 | tf_op jit(solution)/shard_map/while/body/eval_jaxpr/ppermute | solution.py:17
  186.4 8.3 %collective-permute-start = (bf16[2,128,128]{2,1,0:T(8,128)(2,1)S(1)}, bf16[2,128,128]{2,1,0:T(8,128)(2,1)S(1)}, u32[]{:S(2)}, u32[]{:S(2)}) collective-permute-start(bf16[2,128,128]{2,1,0:T(8,128)(2,1)S(1)} %fusion.160), channel_id=1, source_target_pairs={{0,16},{16,32},{32,48},{48,64},{64,80},{80,96},{96,112},{112,128},... | collective-permute-start | bytes 196616 | tf_op jit(solution)/shard_map/while/body/eval_jaxpr/ppermute | solution.py:17
  195.0 8.3 %collective-permute-start = (bf16[2,128,128]{2,1,0:T(8,128)(2,1)S(1)}, bf16[2,128,128]{2,1,0:T(8,128)(2,1)S(1)}, u32[]{:S(2)}, u32[]{:S(2)}) collective-permute-start(bf16[2,128,128]{2,1,0:T(8,128)(2,1)S(1)} %fusion.160), channel_id=1, source_target_pairs={{0,16},{16,32},{32,48},{48,64},{64,80},{80,96},{96,112},{112,128},... | collective-permute-start | bytes 196616 | tf_op jit(solution)/shard_map/while/body/eval_jaxpr/ppermute | solution.py:17
  203.6 8.3 %collective-permute-start = (bf16[2,128,128]{2,1,0:T(8,128)(2,1)S(1)}, bf16[2,128,128]{2,1,0:T(8,128)(2,1)S(1)}, u32[]{:S(2)}, u32[]{:S(2)}) collective-permute-start(bf16[2,128,128]{2,1,0:T(8,128)(2,1)S(1)} %fusion.160), channel_id=1, source_target_pairs={{0,16},{16,32},{32,48},{48,64},{64,80},{80,96},{96,112},{112,128},... | collective-permute-start | bytes 196616 | tf_op jit(solution)/shard_map/while/body/eval_jaxpr/ppermute | solution.py:17
  212.2 8.3 %collective-permute-start = (bf16[2,128,128]{2,1,0:T(8,128)(2,1)S(1)}, bf16[2,128,128]{2,1,0:T(8,128)(2,1)S(1)}, u32[]{:S(2)}, u32[]{:S(2)}) collective-permute-start(bf16[2,128,128]{2,1,0:T(8,128)(2,1)S(1)} %fusion.160), channel_id=1, source_target_pairs={{0,16},{16,32},{32,48},{48,64},{64,80},{80,96},{96,112},{112,128},... | collective-permute-start | bytes 196616 | tf_op jit(solution)/shard_map/while/body/eval_jaxpr/ppermute | solution.py:17
  220.7 8.6 %collective-permute-start = (bf16[2,128,128]{2,1,0:T(8,128)(2,1)S(1)}, bf16[2,128,128]{2,1,0:T(8,128)(2,1)S(1)}, u32[]{:S(2)}, u32[]{:S(2)}) collective-permute-start(bf16[2,128,128]{2,1,0:T(8,128)(2,1)S(1)} %fusion.160), channel_id=1, source_target_pairs={{0,16},{16,32},{32,48},{48,64},{64,80},{80,96},{96,112},{112,128},... | collective-permute-start | bytes 196616 | tf_op jit(solution)/shard_map/while/body/eval_jaxpr/ppermute | solution.py:17
  229.6 8.3 %collective-permute-start = (bf16[2,128,128]{2,1,0:T(8,128)(2,1)S(1)}, bf16[2,128,128]{2,1,0:T(8,128)(2,1)S(1)}, u32[]{:S(2)}, u32[]{:S(2)}) collective-permute-start(bf16[2,128,128]{2,1,0:T(8,128)(2,1)S(1)} %fusion.160), channel_id=1, source_target_pairs={{0,16},{16,32},{32,48},{48,64},{64,80},{80,96},{96,112},{112,128},... | collective-permute-start | bytes 196616 | tf_op jit(solution)/shard_map/while/body/eval_jaxpr/ppermute | solution.py:17
  238.2 8.3 %collective-permute-start = (bf16[2,128,128]{2,1,0:T(8,128)(2,1)S(1)}, bf16[2,128,128]{2,1,0:T(8,128)(2,1)S(1)}, u32[]{:S(2)}, u32[]{:S(2)}) collective-permute-start(bf16[2,128,128]{2,1,0:T(8,128)(2,1)S(1)} %fusion.160), channel_id=1, source_target_pairs={{0,16},{16,32},{32,48},{48,64},{64,80},{80,96},{96,112},{112,128},... | collective-permute-start | bytes 196616 | tf_op jit(solution)/shard_map/while/body/eval_jaxpr/ppermute | solution.py:17
  246.8 8.3 %collective-permute-start = (bf16[2,128,128]{2,1,0:T(8,128)(2,1)S(1)}, bf16[2,128,128]{2,1,0:T(8,128)(2,1)S(1)}, u32[]{:S(2)}, u32[]{:S(2)}) collective-permute-start(bf16[2,128,128]{2,1,0:T(8,128)(2,1)S(1)} %fusion.160), channel_id=1, source_target_pairs={{0,16},{16,32},{32,48},{48,64},{64,80},{80,96},{96,112},{112,128},... | collective-permute-start | bytes 196616 | tf_op jit(solution)/shard_map/while/body/eval_jaxpr/ppermute | solution.py:17
  255.3 8.3 %collective-permute-start = (bf16[2,128,128]{2,1,0:T(8,128)(2,1)S(1)}, bf16[2,128,128]{2,1,0:T(8,128)(2,1)S(1)}, u32[]{:S(2)}, u32[]{:S(2)}) collective-permute-start(bf16[2,128,128]{2,1,0:T(8,128)(2,1)S(1)} %fusion.160), channel_id=1, source_target_pairs={{0,16},{16,32},{32,48},{48,64},{64,80},{80,96},{96,112},{112,128},... | collective-permute-start | bytes 196616 | tf_op jit(solution)/shard_map/while/body/eval_jaxpr/ppermute | solution.py:17
  263.9 8.3 %collective-permute-start = (bf16[2,128,128]{2,1,0:T(8,128)(2,1)S(1)}, bf16[2,128,128]{2,1,0:T(8,128)(2,1)S(1)}, u32[]{:S(2)}, u32[]{:S(2)}) collective-permute-start(bf16[2,128,128]{2,1,0:T(8,128)(2,1)S(1)} %fusion.160), channel_id=1, source_target_pairs={{0,16},{16,32},{32,48},{48,64},{64,80},{80,96},{96,112},{112,128},... | collective-permute-start | bytes 196616 | tf_op jit(solution)/shard_map/while/body/eval_jaxpr/ppermute | solution.py:17
  272.5 8.3 %collective-permute-start = (bf16[2,128,128]{2,1,0:T(8,128)(2,1)S(1)}, bf16[2,128,128]{2,1,0:T(8,128)(2,1)S(1)}, u32[]{:S(2)}, u32[]{:S(2)}) collective-permute-start(bf16[2,128,128]{2,1,0:T(8,128)(2,1)S(1)} %fusion.160), channel_id=1, source_target_pairs={{0,16},{16,32},{32,48},{48,64},{64,80},{80,96},{96,112},{112,128},... | collective-permute-start | bytes 196616 | tf_op jit(solution)/shard_map/while/body/eval_jaxpr/ppermute | solution.py:17
  281.1 8.8 %collective-permute-start = (bf16[2,128,128]{2,1,0:T(8,128)(2,1)S(1)}, bf16[2,128,128]{2,1,0:T(8,128)(2,1)S(1)}, u32[]{:S(2)}, u32[]{:S(2)}) collective-permute-start(bf16[2,128,128]{2,1,0:T(8,128)(2,1)S(1)} %fusion.160), channel_id=1, source_target_pairs={{0,16},{16,32},{32,48},{48,64},{64,80},{80,96},{96,112},{112,128},... | collective-permute-start | bytes 196616 | tf_op jit(solution)/shard_map/while/body/eval_jaxpr/ppermute | solution.py:17
  290.2 8.3 %collective-permute-start = (bf16[2,128,128]{2,1,0:T(8,128)(2,1)S(1)}, bf16[2,128,128]{2,1,0:T(8,128)(2,1)S(1)}, u32[]{:S(2)}, u32[]{:S(2)}) collective-permute-start(bf16[2,128,128]{2,1,0:T(8,128)(2,1)S(1)} %fusion.160), channel_id=1, source_target_pairs={{0,16},{16,32},{32,48},{48,64},{64,80},{80,96},{96,112},{112,128},... | collective-permute-start | bytes 196616 | tf_op jit(solution)/shard_map/while/body/eval_jaxpr/ppermute | solution.py:17
  298.7 8.3 %collective-permute-start = (bf16[2,128,128]{2,1,0:T(8,128)(2,1)S(1)}, bf16[2,128,128]{2,1,0:T(8,128)(2,1)S(1)}, u32[]{:S(2)}, u32[]{:S(2)}) collective-permute-start(bf16[2,128,128]{2,1,0:T(8,128)(2,1)S(1)} %fusion.160), channel_id=1, source_target_pairs={{0,16},{16,32},{32,48},{48,64},{64,80},{80,96},{96,112},{112,128},... | collective-permute-start | bytes 196616 | tf_op jit(solution)/shard_map/while/body/eval_jaxpr/ppermute | solution.py:17
  307.3 8.3 %collective-permute-start = (bf16[2,128,128]{2,1,0:T(8,128)(2,1)S(1)}, bf16[2,128,128]{2,1,0:T(8,128)(2,1)S(1)}, u32[]{:S(2)}, u32[]{:S(2)}) collective-permute-start(bf16[2,128,128]{2,1,0:T(8,128)(2,1)S(1)} %fusion.160), channel_id=1, source_target_pairs={{0,16},{16,32},{32,48},{48,64},{64,80},{80,96},{96,112},{112,128},... | collective-permute-start | bytes 196616 | tf_op jit(solution)/shard_map/while/body/eval_jaxpr/ppermute | solution.py:17
  315.9 8.3 %collective-permute-start = (bf16[2,128,128]{2,1,0:T(8,128)(2,1)S(1)}, bf16[2,128,128]{2,1,0:T(8,128)(2,1)S(1)}, u32[]{:S(2)}, u32[]{:S(2)}) collective-permute-start(bf16[2,128,128]{2,1,0:T(8,128)(2,1)S(1)} %fusion.160), channel_id=1, source_target_pairs={{0,16},{16,32},{32,48},{48,64},{64,80},{80,96},{96,112},{112,128},... | collective-permute-start | bytes 196616 | tf_op jit(solution)/shard_map/while/body/eval_jaxpr/ppermute | solution.py:17
  324.5 8.3 %collective-permute-start = (bf16[2,128,128]{2,1,0:T(8,128)(2,1)S(1)}, bf16[2,128,128]{2,1,0:T(8,128)(2,1)S(1)}, u32[]{:S(2)}, u32[]{:S(2)}) collective-permute-start(bf16[2,128,128]{2,1,0:T(8,128)(2,1)S(1)} %fusion.160), channel_id=1, source_target_pairs={{0,16},{16,32},{32,48},{48,64},{64,80},{80,96},{96,112},{112,128},... | collective-permute-start | bytes 196616 | tf_op jit(solution)/shard_map/while/body/eval_jaxpr/ppermute | solution.py:17
  333.1 8.4 %collective-permute-start = (bf16[2,128,128]{2,1,0:T(8,128)(2,1)S(1)}, bf16[2,128,128]{2,1,0:T(8,128)(2,1)S(1)}, u32[]{:S(2)}, u32[]{:S(2)}) collective-permute-start(bf16[2,128,128]{2,1,0:T(8,128)(2,1)S(1)} %fusion.160), channel_id=1, source_target_pairs={{0,16},{16,32},{32,48},{48,64},{64,80},{80,96},{96,112},{112,128},... | collective-permute-start | bytes 196616 | tf_op jit(solution)/shard_map/while/body/eval_jaxpr/ppermute | solution.py:17
  341.8 8.4 %collective-permute-start = (bf16[2,128,128]{2,1,0:T(8,128)(2,1)S(1)}, bf16[2,128,128]{2,1,0:T(8,128)(2,1)S(1)}, u32[]{:S(2)}, u32[]{:S(2)}) collective-permute-start(bf16[2,128,128]{2,1,0:T(8,128)(2,1)S(1)} %fusion.160), channel_id=1, source_target_pairs={{0,16},{16,32},{32,48},{48,64},{64,80},{80,96},{96,112},{112,128},... | collective-permute-start | bytes 196616 | tf_op jit(solution)/shard_map/while/body/eval_jaxpr/ppermute | solution.py:17
  350.5 8.3 %collective-permute-start = (bf16[2,128,128]{2,1,0:T(8,128)(2,1)S(1)}, bf16[2,128,128]{2,1,0:T(8,128)(2,1)S(1)}, u32[]{:S(2)}, u32[]{:S(2)}) collective-permute-start(bf16[2,128,128]{2,1,0:T(8,128)(2,1)S(1)} %fusion.160), channel_id=1, source_target_pairs={{0,16},{16,32},{32,48},{48,64},{64,80},{80,96},{96,112},{112,128},... | collective-permute-start | bytes 196616 | tf_op jit(solution)/shard_map/while/body/eval_jaxpr/ppermute | solution.py:17
  359.1 8.3 %collective-permute-start = (bf16[2,128,128]{2,1,0:T(8,128)(2,1)S(1)}, bf16[2,128,128]{2,1,0:T(8,128)(2,1)S(1)}, u32[]{:S(2)}, u32[]{:S(2)}) collective-permute-start(bf16[2,128,128]{2,1,0:T(8,128)(2,1)S(1)} %fusion.160), channel_id=1, source_target_pairs={{0,16},{16,32},{32,48},{48,64},{64,80},{80,96},{96,112},{112,128},... | collective-permute-start | bytes 196616 | tf_op jit(solution)/shard_map/while/body/eval_jaxpr/ppermute | solution.py:17
  367.6 8.3 %collective-permute-start = (bf16[2,128,128]{2,1,0:T(8,128)(2,1)S(1)}, bf16[2,128,128]{2,1,0:T(8,128)(2,1)S(1)}, u32[]{:S(2)}, u32[]{:S(2)}) collective-permute-start(bf16[2,128,128]{2,1,0:T(8,128)(2,1)S(1)} %fusion.160), channel_id=1, source_target_pairs={{0,16},{16,32},{32,48},{48,64},{64,80},{80,96},{96,112},{112,128},... | collective-permute-start | bytes 196616 | tf_op jit(solution)/shard_map/while/body/eval_jaxpr/ppermute | solution.py:17
  376.2 8.3 %collective-permute-start = (bf16[2,128,128]{2,1,0:T(8,128)(2,1)S(1)}, bf16[2,128,128]{2,1,0:T(8,128)(2,1)S(1)}, u32[]{:S(2)}, u32[]{:S(2)}) collective-permute-start(bf16[2,128,128]{2,1,0:T(8,128)(2,1)S(1)} %fusion.160), channel_id=1, source_target_pairs={{0,16},{16,32},{32,48},{48,64},{64,80},{80,96},{96,112},{112,128},... | collective-permute-start | bytes 196616 | tf_op jit(solution)/shard_map/while/body/eval_jaxpr/ppermute | solution.py:17
  488.7 2.0 copy-start.4
  488.7 2.8 copy-start.15
  490.4 2.4 copy-start.14
Sparse Core Ops, SparseCore 0:
  502.6 60.9 reduce-scatter.3
where the time goes:
time: 578 us; the launch traced here: 572 us
  waiting for transfers between devices  262 us (45%)
  matrix products  178 us (31%)
  starting transfers between devices  61.9 us (11%)
  local copies, waits for them, and re-layouts  45 us (8%)
  between operations  13.9 us (2%)
  other arithmetic  8.47 us (1%)
    ppermute x31, waiting for transfers between devices, shifted(): return lax.ppermute(block, axis, route)  201 us
    ppermute x31, starting transfers between devices, shifted(): return lax.ppermute(block, axis, route)  61.9 us
    unnamed x2, waiting for transfers between devices  61.2 us
    dot_general x16, matrix products, block_step(): output = terms + jnp.matmul(scores, write_vals, precision=highest)  26.6 us
    dot_general x16, matrix products, block_step(): jnp.einsum('...cv,...ck->...vk', tail_keep[..., None] * fresh_vals, keys,...  21.3 us
    dot_general x16, matrix products, fold_blocks(): jnp.matmul(total_state, move_now, precision=highest) + carried_now  20.8 us
    dot_general x16, matrix products, fold_blocks(): next_move = jnp.matmul(total_move, move_now, precision=highest)  20.8 us
    dot_general x16, matrix products, state_terms(): jnp.einsum('...ck,...vk->...cv', erase_keys, states, precision=highest)  19.3 us
  transfers between devices with their start and end apart: 32, of which 32 were waited for; matrix products, arithmetic and copies ran while one was open for 0% of the time, Pallas kernels for 0%

commit v1 on v0

v1 whole, which is shorter than its diff:
```python
import jax
import jax.numpy as jnp
from jax import lax
from jax.experimental import pallas as pl
from jax.experimental.pallas import tpu as pltpu
from jax.sharding import PartitionSpec as P

W = 128
NX, NZ, NY = 4, 8, 8
MSG_ROWS = W + 16
PIECES = 4
f32, bf16 = jnp.float32, jnp.bfloat16
MESH = pl.DeviceIdType.MESH


def dot(a, b):
    return jnp.dot(a, b, preferred_element_type=f32)


def dot_t(a, b):
    return lax.dot_general(a, b, (((1,), (1,)), ((), ())), preferred_element_type=f32)


def split3(x):
    hi = x.astype(bf16)
    rest = x - hi.astype(f32)
    mid = rest.astype(bf16)
    low = (rest - mid.astype(f32)).astype(bf16)
    return hi, mid, low


def local_kernel(
    q_ref, k_ref, v_ref, rate_ref, log_ref, start_ref, qeff_ref, att_ref, msg_ref, rows, cols, y_ref, gam_ref
):
    chunks = q_ref.shape[0] // W
    row = lax.broadcasted_iota(jnp.int32, (W, W), 0)
    col = lax.broadcasted_iota(jnp.int32, (W, W), 1)
    lower = row >= col
    eye = row == col

    rows[...] = jnp.zeros_like(rows)
    for c in range(chunks):
        here = slice(c * W, (c + 1) * W)
        rows[8 * c : 8 * c + 2, :] = log_ref[:, here]
        rows[8 * c + 2 : 8 * c + 3, :] = start_ref[c : c + 1, :].astype(f32)
        rows[8 * c + 3 : 8 * c + 5, :] = rate_ref[:, here]
    raw = rows[...]
    upper = (row <= col).astype(f32)
    summed = jnp.dot(raw, upper, precision=lax.Precision.HIGHEST, preferred_element_type=f32)
    kind = lax.broadcasted_iota(jnp.int32, raw.shape, 0) % 8
    vectors = jnp.where(kind < 3, summed, raw)
    rows[...] = vectors
    turned = jnp.transpose(vectors)
    for c in range(chunks):
        cols[c] = turned[:, 8 * c : 8 * c + 8]

    y_ref[...] = jnp.zeros_like(y_ref)
    gam_ref[...] = jnp.ones_like(gam_ref)

    def prepare(c):
        start = pl.multiple_of(c * W, W)
        kc = k_ref[pl.ds(start, W), :]
        qc = q_ref[pl.ds(start, W), :]
        vc = v_ref[pl.ds(start, W), :]
        vec_r = rows[pl.ds(pl.multiple_of(c * 8, 8), 8), :]
        vec_c = cols[c]
        kf = kc.astype(f32)
        qf = qc.astype(f32)
        rk_c = lax.rsqrt(jnp.sum(kf * kf, axis=1, keepdims=True) + 1e-6)
        rq_c = lax.rsqrt(jnp.sum(qf * qf, axis=1, keepdims=True) + 1e-6)
        rk_r = jnp.sum(jnp.where(eye, rk_c, 0.0), axis=0, keepdims=True)
        kk = dot_t(kc, kc) * rk_c * rk_r
        qk = dot_t(qc, kc) * rq_c * rk_r
        k_turned = jnp.transpose(kf).astype(bf16)
        reset_r, reset_c = vec_r[2:3], vec_c[:, 2:3]
        same = lower & (reset_r == reset_c)
        reset_last = reset_r[:, W - 1 : W]
        found = []
        for h in range(2):
            g_r, g_c = vec_r[h : h + 1], vec_c[:, h : h + 1]
            b_r, b_c = vec_r[3 + h : 4 + h], vec_c[:, 3 + h : 4 + h]
            g_last = g_r[:, W - 1 : W]
            decay = jnp.exp(jnp.where(same, g_c - g_r, -1e9))
            coupling = b_c * kk * decay
            inverse = jnp.where(eye, 1.0, jnp.where((row // 2 == col // 2) & lower, -coupling, 0.0))
            found.append([decay, coupling, inverse])
        size = 2
        while size < W:
            block = (row // (2 * size) == col // (2 * size)) & (row // size > col // size)
            for h in range(2):
                decay, coupling, inverse = found[h]
                inv_b = inverse.astype(bf16)
                part = dot(jnp.where(block, coupling, 0.0).astype(bf16), inv_b)
                found[h][2] = inverse - dot(inv_b, part.astype(bf16))
            size *= 2
        results = []
        for h in range(2):
            decay, coupling, inverse = found[h]
            g_r, g_c = vec_r[h : h + 1], vec_c[:, h : h + 1]
            b_r = vec_r[3 + h : 4 + h]
            g_last = g_r[:, W - 1 : W]
            head_r = jnp.where(reset_r == 0.0, jnp.exp(g_r), 0.0)
            head_c = jnp.where(reset_c == 0.0, jnp.exp(g_c), 0.0)
            tail_c = jnp.where(reset_c == reset_last, jnp.exp(g_last - g_c), 0.0)
            whole = jnp.where(reset_last == 0.0, jnp.exp(g_last), 0.0)
            erase = dot((inverse * (b_r * head_r * rk_r)).astype(bf16), kc)
            write = dot((inverse * b_r).astype(bf16), vc[:, h * W : (h + 1) * W])
            both = jnp.concatenate([erase, write], axis=1)
            score = (qk * decay).astype(bf16)
            scored = dot(score, both.astype(bf16))
            reach = qf * (head_c * rq_c) - scored[:, :W]
            moved = dot(k_turned, (both * (tail_c * rk_c)).astype(bf16))
            results.append((reach, scored[:, W:], moved[:, :W], moved[:, W:], whole))
        return results

    def advance(c, results):
        start = pl.multiple_of(c * W, W)
        for h in range(2):
            reach, local_out, fade, fresh, whole = results[h]
            y = y_ref[h]
            gam = gam_ref[h, 0:1, 0:1]
            stacked = jnp.concatenate([fade, reach], axis=0).astype(bf16)
            product = dot(stacked, y.astype(bf16))
            qeff_ref[pl.ds(start, W), h * W : (h + 1) * W] = (
                product[W:, :W] + gam * reach
            ).astype(bf16)
            att_ref[pl.ds(start, W), h * W : (h + 1) * W] = product[W:, W:] + local_out
            y_ref[h] = whole * y - product[:W] + jnp.concatenate([-gam * fade, fresh], axis=1)
            gam_ref[h] = gam_ref[h] * whole

    def body(i, carry):
        ready = [prepare(2 * i), prepare(2 * i + 1)]
        for j in range(2):
            advance(2 * i + j, ready[j])
        return carry

    lax.fori_loop(0, chunks // 2, body, 0)
    for h in range(2):
        msg_ref[h, :W, :] = y_ref[h].astype(bf16)
        gam = jnp.broadcast_to(gam_ref[h, 0:1, 0:1], (16, 2 * W))
        hi, mid, low = split3(gam)
        at = lax.broadcasted_iota(jnp.int32, (16, 2 * W), 0)
        msg_ref[h, W:, :] = jnp.where(
            at == 0, hi.astype(f32), jnp.where(at == 1, mid.astype(f32), jnp.where(at == 2, low.astype(f32), 0.0))
        ).astype(bf16)


def local_part(queries, keys, values, rates, logs, starts):
    tokens = queries.shape[0]
    chunks = tokens // W
    return pl.pallas_call(
        local_kernel,
        out_shape=(
            jax.ShapeDtypeStruct((tokens, 2 * W), bf16),
            jax.ShapeDtypeStruct((tokens, 2 * W), f32),
            jax.ShapeDtypeStruct((2, MSG_ROWS, 2 * W), bf16),
        ),
        in_specs=[pl.BlockSpec(memory_space=pltpu.VMEM)] * 6,
        out_specs=(pl.BlockSpec(memory_space=pltpu.VMEM),) * 3,
        scratch_shapes=[
            pltpu.VMEM((8 * chunks, W), f32),
            pltpu.VMEM((chunks, W, 8), f32),
            pltpu.VMEM((2, W, 2 * W), f32),
            pltpu.VMEM((2, 8, W), f32),
        ],
        compiler_params=pltpu.CompilerParams(vmem_limit_bytes=32 << 20),
    )(queries, keys, values, rates, logs, starts)


def far_kernel(
    sizes, qeff_ref, att_ref, msg_ref, gate_ref, gain_ref, w_ref, out_ref,
    got, before, hop_out, hop_in, weights, normed, sent, came,
    right_s, right_r, left_s, left_r, hop_s, hop_r, w_own, w_s, w_r, n_s, n_r, ring_s, ring_r,
):
    nx, nz, ny = sizes
    seq, head = lax.axis_index("seq"), lax.axis_index("head")
    x, z = seq // nz, lax.rem(seq, nz)
    y, core = head // 2, lax.rem(head, 2)
    half = nz // 2
    step_y = 1 - 2 * core

    def seq_of(x_at, z_at):
        return lax.rem(x_at + nx, nx) * nz + lax.rem(z_at + nz, nz)

    def head_of(y_at, core_at):
        return lax.rem(y_at + ny, ny) * 2 + core_at

    above, below = (seq_of(x, z + 1), head), (seq_of(x, z - 1), head)
    next_row, last_row = (seq_of(x + 1, z), head), (seq_of(x - 1, z), head)
    sibling = (seq, head_of(y, 1 - core))
    ahead, behind = (seq, head_of(y + 1, core)), (seq, head_of(y - 1, core))
    target = (seq, head_of(y + step_y, core))

    barrier = pltpu.get_barrier_semaphore()
    greeted = (above, below, next_row, last_row, sibling, ahead, behind)
    for other in greeted:
        pl.semaphore_signal(barrier, inc=1, device_id=other, device_id_type=MESH)
    pl.semaphore_wait(barrier, len(greeted))

    def remote(src, dst, send, recv, device):
        return pltpu.make_async_remote_copy(
            src_ref=src, dst_ref=dst, send_sem=send, recv_sem=recv, device_id=device, device_id_type=MESH
        )

    def around(t, h, upward):
        owner = lax.rem(z - t + nz, nz) if upward else lax.rem(z + t, nz)
        src = msg_ref.at[h] if t == 0 else got.at[owner, h]
        if upward:
            return remote(src, got.at[owner, h], right_s.at[t, h], right_r.at[t, h], above)
        return remote(src, got.at[owner, h], left_s.at[t, h], left_r.at[t, h], below)

    def wanted(t, h, upward):
        return t < half - 1 or h == (0 if upward else 1)

    for h in range(2):
        for upward in (True, False):
            if wanted(0, h, upward):
                around(0, h, upward).start()

    def weight_copies(d):
        mine = pl.ds(pl.multiple_of((2 * d + core) * W, W), W)
        theirs = pl.ds(pl.multiple_of((2 * d + 1 - core) * W, W), W)
        own = pltpu.make_async_copy(w_ref.at[:, mine], weights.at[d, : 2 * W], w_own.at[d])
        far = remote(w_ref.at[:, theirs], weights.at[d, 2 * W :], w_s.at[d], w_r.at[d], sibling)
        return own, far

    for d in range(ny):
        own, far = weight_copies(d)
        own.start()
        far.start()

    got[z] = msg_ref[...]
    for t in range(1, half):
        for h in range(2):
            for upward in (True, False):
                if wanted(t - 1, h, upward):
                    around(t - 1, h, upward).wait_recv()
                if wanted(t, h, upward):
                    around(t, h, upward).start()
    for h in range(2):
        for upward in (True, False):
            if wanted(half - 1, h, upward):
                around(half - 1, h, upward).wait_recv()

    def gamma_of(rows16):
        return jnp.sum(rows16.astype(f32), axis=0, keepdims=True)

    total = [jnp.zeros((W, 2 * W), f32)] * 2
    gammas = [jnp.ones((1, 2 * W), f32)] * 2
    for at in range(nz):
        for h in range(2):
            before[at, h, :W] = total[h]
            before[at, h, W : W + 8] = jnp.broadcast_to(gammas[h], (8, 2 * W))
            theirs = got[at, h, :W].astype(f32)
            shrink = gamma_of(got[at, h, W:])
            term = jnp.concatenate([gammas[h][:, :W] * theirs[:, :W], theirs[:, W:]], axis=1)
            if at == 0:
                total[h] = term
            else:
                total[h] = (
                    shrink * total[h] + dot(got[at, h, :W, :W], total[h].astype(bf16)) + term
                )
            gammas[h] = gammas[h] * shrink

    def hop(h):
        return remote(hop_out.at[h], hop_in.at[h], hop_s.at[h], hop_r.at[h], next_row)

    @pl.when(x == 0)
    def _():
        hop_in[...] = jnp.zeros_like(hop_in)

    entering = []
    for h in range(2):
        @pl.when(x > 0)
        def _():
            hop(h).wait_recv()

        came_in = hop_in[h]
        wide = came_in.astype(f32)

        @pl.when(x < nx - 1)
        def _():
            hop_out[h] = (
                gammas[h][:, :W] * wide + dot(total[h][:, :W].astype(bf16), came_in) + total[h][:, W:]
            ).astype(bf16)
            hop(h).start()

        prefix = before[z, h, :W]
        kept = before[z, h, W : W + 1]
        entering.append(
            (kept[:, :W] * wide + dot(prefix[:, :W].astype(bf16), came_in) + prefix[:, W:]).astype(bf16)
        )

    pieces = PIECES
    size = qeff_ref.shape[0] // pieces
    gain = gain_ref[...]

    def normed_copy(p):
        return remote(normed.at[0, p], normed.at[1, p], n_s.at[p], n_r.at[p], sibling)

    def make_normed(p):
        here = slice(p * size, (p + 1) * size)
        for h in range(2):
            lanes = slice(h * W, (h + 1) * W)
            attended = att_ref[here, lanes] + dot(qeff_ref[here, lanes], entering[h])
            scale = lax.rsqrt(jnp.mean(attended * attended, axis=1, keepdims=True) + 1e-6)
            gate = gate_ref[here, lanes].astype(f32)
            normed[0, p, :, lanes] = (attended * scale * gain * (gate / (1.0 + jnp.exp(-gate)))).astype(bf16)

    def partial(p, d):
        return dot(normed[0, p], weights[d, : 2 * W]) + dot(normed[1, p], weights[d, 2 * W :])

    def ring(s, p):
        return remote(sent.at[s, p], came.at[s, p], ring_s.at[s, p], ring_r.at[s, p], target)

    def block_of(s):
        return lax.rem(y - step_y * (s + 1) + 2 * ny, ny)

    def first_step(p):
        normed_copy(p).wait_recv()
        sent[0, p] = partial(p, block_of(0)).astype(bf16)
        ring(0, p).start()

    for p in range(pieces):
        make_normed(p)
        normed_copy(p).start()
        if p == 0:
            for d in range(ny):
                own, far = weight_copies(d)
                own.wait()
                far.wait_recv()
        if p > 0:
            first_step(p - 1)
    first_step(pieces - 1)

    def step(s, carry):
        d = block_of(s)
        for p in range(pieces):
            mine = partial(p, d)
            ring(s - 1, p).wait_recv()
            sent[s, p] = (mine + came[s - 1, p].astype(f32)).astype(bf16)
            ring(s, p).start()
        return carry

    lax.fori_loop(1, ny - 1, step, 0)
    for p in range(pieces):
        mine = partial(p, y)
        ring(ny - 2, p).wait_recv()
        out_ref[p * size : (p + 1) * size, :] = (mine + came[ny - 2, p].astype(f32)).astype(bf16)

    for t in range(half):
        for h in range(2):
            for upward in (True, False):
                if wanted(t, h, upward):
                    around(t, h, upward).wait_send()
    for d in range(ny):
        weight_copies(d)[1].wait_send()
    for h in range(2):
        @pl.when(x < nx - 1)
        def _():
            hop(h).wait_send()
    for p in range(pieces):
        normed_copy(p).wait_send()

    def drain(s, carry):
        for p in range(pieces):
            ring(s, p).wait_send()
        return carry

    lax.fori_loop(0, ny - 1, drain, 0)


def far_part(sizes, qeff, att, msg, gate, gain, weight):
    nx, nz, ny = sizes
    tokens = qeff.shape[0]
    half = nz // 2
    size = tokens // PIECES
    vmem = pl.BlockSpec(memory_space=pltpu.VMEM)
    dma = pltpu.SemaphoreType.DMA

    def kernel(*refs):
        far_kernel(sizes, *refs)

    return pl.pallas_call(
        kernel,
        out_shape=jax.ShapeDtypeStruct((tokens, W), bf16),
        in_specs=[vmem, vmem, vmem, vmem, vmem, pl.BlockSpec(memory_space=pl.ANY)],
        out_specs=vmem,
        scratch_shapes=[
            pltpu.VMEM((nz, 2, MSG_ROWS, 2 * W), bf16),
            pltpu.VMEM((nz, 2, W + 8, 2 * W), f32),
            pltpu.VMEM((2, W, W), bf16),
            pltpu.VMEM((2, W, W), bf16),
            pltpu.VMEM((ny, 4 * W, W), bf16),
            pltpu.VMEM((2, PIECES, size, 2 * W), bf16),
            pltpu.VMEM((ny - 1, PIECES, size, W), bf16),
            pltpu.VMEM((ny - 1, PIECES, size, W), bf16),
            dma((half, 2)), dma((half, 2)), dma((half, 2)), dma((half, 2)),
            dma((2,)), dma((2,)),
            dma((ny,)), dma((ny,)), dma((ny,)),
            dma((PIECES,)), dma((PIECES,)),
            dma((ny - 1, PIECES)), dma((ny - 1, PIECES)),
        ],
        compiler_params=pltpu.CompilerParams(
            collective_id=0, has_side_effects=True, vmem_limit_bytes=48 << 20
        ),
    )(qeff, att, msg, gate, gain, weight)


def build(mesh, sizes):
    def local(queries, keys, values, gate, rates, logs, starts, gain, weight):
        qeff, att, msg = local_part(
            queries, keys, values, rates, logs, starts.reshape(-1, W)
        )
        return far_part(sizes, qeff, att, msg, gate, gain.reshape(1, W), weight)

    both = P("seq", "head")
    placed = (both, both, both, both, P("head", "seq"), P("head", "seq"), P("seq"), P(), P("head", None))
    return jax.shard_map(local, mesh=mesh, in_specs=placed, out_specs=both, check_vma=False)


def solution(mesh):
    return build(mesh, (NX, NZ, NY))
```

time: 578 us -> 94.6 us (0.16)
  waiting for transfers between devices: 262 us -> 0 us
  matrix products: 178 us -> 0 us
  Pallas kernels: 0 us -> 86.7 us
  starting transfers between devices: 61.9 us -> 0 us
  local copies, waits for them, and re-layouts: 45 us -> 7.5 us
  between operations: 13.9 us -> 0.04 us
  other arithmetic: 8.47 us -> 0 us
    ppermute x31 -> x0, waiting for transfers between devices: 201 us -> none  [shifted(): return lax.ppermute(block, axis, route)]
    dot_general x160 -> x0, matrix products: 178 us -> none  [the longest x16 26.6 us: block_step(): output = terms + jnp.matmul(scores, write_vals, precision=highest)]
    pallas_call x0 -> x2, Pallas kernels: none -> 86.7 us  [the longest x1 67.3 us: far_part(): pl.pallas_call(kernel, out_shape=jax.ShapeDtypeStruct((tokens, W), bf16),...]
    ppermute x31 -> x0, starting transfers between devices: 61.9 us -> none  [shifted(): return lax.ppermute(block, axis, route)]
    unnamed x2 -> x0, waiting for transfers between devices: 61.2 us -> none
    dynamic_slice x48 -> x0, local copies, waits for them, and re-layouts: 16.5 us -> none  [the longest x32 16.3 us: local(): lax.scan(fold_blocks, (eye_heads, empty), (blocks_first(moves), blocks_fi...]
    mul x19 -> x0, local copies, waits for them, and re-layouts: 13.1 us -> none  [the longest x16 11.1 us: block_step(): whole_keep[..., None, None] * state_now]
  transfers between devices with their start and end apart: 32 -> 0, of which waited for: 32 -> 0; matrix products, arithmetic and copies ran while one was open for 0% -> 0% of each run, Pallas kernels for 0% -> 0%
where the time goes in v1:
time: 94.6 us; the launch traced here: 94.3 us
  Pallas kernels  86.7 us (92%)
  local copies, waits for them, and re-layouts  7.5 us (8%)
    pallas_call x1, Pallas kernels, far_part(): pl.pallas_call(kernel, out_shape=jax.ShapeDtypeStruct((tokens, W), bf16),...  67.3 us
    pallas_call x1, Pallas kernels, local_part(): pl.pallas_call(local_kernel, out_shape=(jax.ShapeDtypeStruct((tokens, 2 *...  19.4 us
    unnamed x19, local copies, waits for them, and re-layouts  7.5 us

profile of v1, /device:TPU:6, one launch (start us, length us, event | category | flops | bytes accessed | tf_op | source)
XLA Modules:
  0.0 94.3 jit_solution(15104989543380287940)
XLA Ops:
  0.0 0.0 copy-start
  0.0 0.0 copy-start.1
  0.0 1.1 %copy-done.1 = bf16[1024,256]{1,0:T(8,128)(2,1)S(1)} copy-done((bf16[1024,256]{1,0:T(8,128)(2,1)S(1)}, bf16[1024,256]{1,0:T(8,128)(2,1)}, u32[]{:S(2)}) %copy-start.1) | copy-done | bytes 524312
  1.1 0.0 copy-start.3
  1.1 0.9 %copy-done.3 = bf16[1024,128]{1,0:T(8,128)(2,1)S(1)} copy-done((bf16[1024,128]{1,0:T(8,128)(2,1)S(1)}, bf16[1024,128]{1,0:T(8,128)(2,1)}, u32[]{:S(2)}) %copy-start.3) | copy-done | bytes 262168
  2.1 0.0 copy-start.4
  2.1 0.9 %copy-done.4 = bf16[1024,128]{1,0:T(8,128)(2,1)S(1)} copy-done((bf16[1024,128]{1,0:T(8,128)(2,1)S(1)}, bf16[1024,128]{1,0:T(8,128)(2,1)}, u32[]{:S(2)}) %copy-start.4) | copy-done | bytes 262168
  3.0 0.0 copy-start.5
  3.0 0.7 copy-done.5
  3.7 0.0 copy-start.6
  3.7 0.7 copy-done.6
  4.4 0.0 copy-start.7
  4.4 0.7 copy-done.7
  5.1 19.4 %shard_map.91 = (bf16[1024,256]{1,0:T(8,128)(2,1)S(1)}, f32[1024,256]{1,0:T(8,128)S(1)}, bf16[2,144,256]{2,1,0:T(8,128)(2,1)S(1)}) custom-call(bf16[1024,128]{1,0:T(8,128)(2,1)S(1)} %copy-done.3, bf16[1024,128]{1,0:T(8,128)(2,1)S(1)} %copy-done.4, bf16[1024,256]{1,0:T(8,128)(2,1)S(1)} %copy-done.1, f32[2,1024]{1,0:T(2,128)S(1)} %copy-done.5, ...), custom_call_target="tpu_custom_call" | custom-call | tf_op jit(solution)/shard_map/pallas_call | solution.py:151
  24.5 0.0 copy-start.8
  24.5 0.0 copy-done
  24.5 0.6 copy-done.8
  25.2 0.0 copy-start.2
  25.2 1.0 %copy-done.2 = bf16[1024,256]{1,0:T(8,128)(2,1)S(1)} copy-done((bf16[1024,256]{1,0:T(8,128)(2,1)S(1)}, bf16[1024,256]{1,0:T(8,128)(2,1)}, u32[]{:S(2)}) %copy-start.2) | copy-done | bytes 524312
  26.2 67.3 %shard_map.92 = bf16[1024,128]{1,0:T(8,128)(2,1)S(1)} custom-call(bf16[1024,256]{1,0:T(8,128)(2,1)S(1)} %get-tuple-element.8.refs_0_, f32[1024,256]{1,0:T(8,128)S(1)} %get-tuple-element.9.refs_1_, bf16[2,144,256]{2,1,0:T(8,128)(2,1)S(1)} %get-tuple-element.10.refs_2_, bf16[1024,256]{1,0:T(8,128)(2,1)S(1)} %copy-done.2, f32[1,128]{1,0:T(1,128)S(1)} %bitcast.3, ...), custom_call_target="tpu_custom_call" | custom-call | tf_op jit(solution)/shard_map/pallas_call | solution.py:384
  93.6 0.7 copy.11
Async XLA Ops:
  0.0 24.5 %copy-start = (bf16[256,2048]{1,0:T(8,128)(2,1)S(1)}, bf16[256,2048]{1,0:T(8,128)(2,1)}, u32[]{:S(2)}) copy-start(bf16[256,2048]{1,0:T(8,128)(2,1)} %refs_5_.1) | copy-start | bytes 3145732
  0.0 1.1 %copy-start.1 = (bf16[1024,256]{1,0:T(8,128)(2,1)S(1)}, bf16[1024,256]{1,0:T(8,128)(2,1)}, u32[]{:S(2)}) copy-start(bf16[1024,256]{1,0:T(8,128)(2,1)} %v_ref.1) | copy-start | bytes 1572868
  1.1 0.9 %copy-start.3 = (bf16[1024,128]{1,0:T(8,128)(2,1)S(1)}, bf16[1024,128]{1,0:T(8,128)(2,1)}, u32[]{:S(2)}) copy-start(bf16[1024,128]{1,0:T(8,128)(2,1)} %q_ref.1) | copy-start | bytes 786436
  2.1 0.9 %copy-start.4 = (bf16[1024,128]{1,0:T(8,128)(2,1)S(1)}, bf16[1024,128]{1,0:T(8,128)(2,1)}, u32[]{:S(2)}) copy-start(bf16[1024,128]{1,0:T(8,128)(2,1)} %k_ref.1) | copy-start | bytes 786436
  3.0 0.7 copy-start.5
  3.7 0.7 copy-start.6
  4.4 0.7 copy-start.7
  24.5 0.7 copy-start.8
  25.2 1.0 %copy-start.2 = (bf16[1024,256]{1,0:T(8,128)(2,1)S(1)}, bf16[1024,256]{1,0:T(8,128)(2,1)}, u32[]{:S(2)}) copy-start(bf16[1024,256]{1,0:T(8,128)(2,1)} %refs_3_.1) | copy-start | bytes 1572868

commit v2 on v1

v2 whole, which is shorter than its diff:
```python
import jax
import jax.numpy as jnp
from jax import lax
from jax.experimental import pallas as pl
from jax.experimental.pallas import tpu as pltpu
from jax.sharding import PartitionSpec as P

W = 128
NX, NZ, NY = 4, 8, 8
PIECES = 4
GROUP = 4
f32, bf16 = jnp.float32, jnp.bfloat16
MESH = pl.DeviceIdType.MESH


def dot(a, b):
    return jnp.dot(a, b, preferred_element_type=f32)


def dot_t(a, b):
    return lax.dot_general(a, b, (((1,), (1,)), ((), ())), preferred_element_type=f32)


def compose(later, earlier):
    g2, y2 = later
    g1, y1 = earlier
    term = jnp.concatenate([g1 * y2[:, :W], y2[:, W:]], axis=1)
    return g1 * g2, g2 * y1 + dot(y2[:, :W].astype(bf16), y1.astype(bf16)) + term


def iotas():
    return lax.broadcasted_iota(jnp.int32, (W, W), 0), lax.broadcasted_iota(jnp.int32, (W, W), 1)


def gather_vectors(q_ref, k_ref, rate_ref, log_ref, start_ref, rows, cols):
    chunks = k_ref.shape[0] // W
    row, col = iotas()
    eye = row == col
    rows[...] = jnp.zeros_like(rows)
    for c in range(chunks):
        here = slice(c * W, (c + 1) * W)
        rows[8 * c : 8 * c + 2, :] = log_ref[:, here]
        rows[8 * c + 2 : 8 * c + 3, :] = start_ref[c : c + 1, :].astype(f32)
        rows[8 * c + 3 : 8 * c + 5, :] = rate_ref[:, here]
    raw = rows[...]
    upper = (row <= col).astype(f32)
    summed = jnp.dot(raw, upper, precision=lax.Precision.HIGHEST, preferred_element_type=f32)
    kind = lax.broadcasted_iota(jnp.int32, raw.shape, 0) % 8
    vectors = jnp.where(kind < 3, summed, raw)
    rows[...] = vectors
    turned = jnp.transpose(vectors)
    lane = lax.broadcasted_iota(jnp.int32, (W, 8), 1)
    for c in range(chunks):
        here = slice(c * W, (c + 1) * W)
        kf = k_ref[here, :].astype(f32)
        qf = q_ref[here, :].astype(f32)
        rk_c = lax.rsqrt(jnp.sum(kf * kf, axis=1, keepdims=True) + 1e-6)
        rq_c = lax.rsqrt(jnp.sum(qf * qf, axis=1, keepdims=True) + 1e-6)
        rows[8 * c + 5 : 8 * c + 6, :] = jnp.sum(jnp.where(eye, rk_c, 0.0), axis=0, keepdims=True)
        cols[c] = jnp.where(lane == 5, rk_c, jnp.where(lane == 6, rq_c, turned[:, 8 * c : 8 * c + 8]))


def chunk_at(ref, c):
    return ref[pl.ds(pl.multiple_of(c * W, W), W), :]


def vectors_at(rows, cols, c):
    return rows[pl.ds(pl.multiple_of(c * 8, 8), 8), :], cols[c]


def decay_of(vec_r, vec_c, h):
    row, col = iotas()
    same = (row >= col) & (vec_r[2:3] == vec_c[:, 2:3])
    return jnp.exp(jnp.where(same, vec_c[:, h : h + 1] - vec_r[h : h + 1], -1e9))


def odd_rows(values, size):
    return jnp.concatenate([values[at : at + size] for at in range(size, W, 2 * size)], axis=0)


def refine(inverse, coupling, size):
    if size < 8:
        row, col = iotas()
        block = (row // (2 * size) == col // (2 * size)) & (row // size > col // size)
        inv_b = inverse.astype(bf16)
        part = dot(jnp.where(block, coupling, 0.0).astype(bf16), inv_b)
        return inverse - dot(inv_b, part.astype(bf16))
    row = lax.broadcasted_iota(jnp.int32, (W // 2, W), 0)
    col = lax.broadcasted_iota(jnp.int32, (W // 2, W), 1)
    block = 2 * (row // size) == col // size
    left = jnp.where(block, odd_rows(coupling, size), 0.0).astype(bf16)
    part = dot(left, inverse.astype(bf16))
    zeros = jnp.zeros((size, W), f32)
    spread = []
    for at in range(0, W // 2, size):
        spread += [zeros, part[at : at + size]]
    odd = odd_rows(inverse, size)
    odd = odd - dot(odd.astype(bf16), jnp.concatenate(spread, axis=0).astype(bf16))
    mixed = []
    for at in range(0, W // 2, size):
        mixed += [inverse[2 * at : 2 * at + size], odd[at : at + size]]
    return jnp.concatenate(mixed, axis=0)


def shard_map_of(h, i, first, k_ref, v_ref, rows, cols, kk_ref, kt_ref, both_ref, maps_ref, total_ref, gam_ref):
    row, col = iotas()
    found = []
    for j in range(GROUP):
        c = GROUP * i + j
        vec_r, vec_c = vectors_at(rows, cols, c)
        if first:
            kc = chunk_at(k_ref, c)
            kk = dot_t(kc, kc) * vec_c[:, 5:6] * vec_r[5:6]
            kk_ref[c] = kk
            kt_ref[c] = jnp.transpose(kc.astype(f32)).astype(bf16)
        else:
            kk = kk_ref[c]
        coupling = vec_c[:, 3 + h : 4 + h] * kk * decay_of(vec_r, vec_c, h)
        near = jnp.where((row // 2 == col // 2) & (row >= col), -coupling, 0.0)
        found.append([coupling, jnp.where(row == col, 1.0, near)])
    size = 2
    while size < W:
        for j in range(GROUP):
            found[j][1] = refine(found[j][1], found[j][0], size)
        size *= 2
    moves = []
    for j in range(GROUP):
        c = GROUP * i + j
        inverse = found[j][1]
        vec_r, vec_c = vectors_at(rows, cols, c)
        g_r, g_c, b_r, rk_r = vec_r[h : h + 1], vec_c[:, h : h + 1], vec_r[3 + h : 4 + h], vec_r[5:6]
        reset_r, reset_c = vec_r[2:3], vec_c[:, 2:3]
        g_last, reset_last = g_r[:, W - 1 : W], reset_r[:, W - 1 : W]
        head_r = jnp.where(reset_r == 0.0, jnp.exp(g_r), 0.0)
        tail_c = jnp.where(reset_c == reset_last, jnp.exp(g_last - g_c), 0.0)
        whole = jnp.where(reset_last == 0.0, jnp.exp(g_last), 0.0)
        erase = dot((inverse * (b_r * head_r * rk_r)).astype(bf16), chunk_at(k_ref, c))
        values = v_ref[pl.ds(pl.multiple_of(c * W, W), W), h * W : (h + 1) * W]
        write = dot((inverse * b_r).astype(bf16), values)
        both = jnp.concatenate([erase, write], axis=1)
        both_ref[c, h] = both.astype(bf16)
        moves.append((whole, dot(kt_ref[c], (both * (tail_c * vec_c[:, 5:6])).astype(bf16))))
    total, gam = total_ref[h], gam_ref[h, 0:1, :]
    for j in range(GROUP):
        c = GROUP * i + j
        whole, moved = moves[j]
        total_b = total.astype(bf16)
        maps_ref[c, h] = total_b
        gam_ref[h, pl.ds(8 + c, 1), :] = gam
        total = (
            whole * total
            - dot(moved[:, :W].astype(bf16), total_b)
            + jnp.concatenate([-gam * moved[:, :W], moved[:, W:]], axis=1)
        )
        gam = gam * whole
    total_ref[h] = total
    gam_ref[h, 0:1, :] = gam


def token_outputs(c, q_ref, k_ref, rows, cols, both_ref, maps_ref, gam_ref, qeff_ref, att_ref):
    start = pl.multiple_of(c * W, W)
    vec_r, vec_c = vectors_at(rows, cols, c)
    qc = chunk_at(q_ref, c)
    qk = dot_t(qc, chunk_at(k_ref, c)) * vec_c[:, 6:7] * vec_r[5:6]
    for h in range(2):
        both = both_ref[c, h]
        g_c, reset_c = vec_c[:, h : h + 1], vec_c[:, 2:3]
        head_c = jnp.where(reset_c == 0.0, jnp.exp(g_c), 0.0)
        scored = dot((qk * decay_of(vec_r, vec_c, h)).astype(bf16), both)
        reach = qc.astype(f32) * (head_c * vec_c[:, 6:7]) - scored[:, :W]
        product = dot(reach.astype(bf16), maps_ref[c, h])
        lanes = slice(h * W, (h + 1) * W)
        gam = gam_ref[h, pl.ds(8 + c, 1), :]
        qeff_ref[pl.ds(start, W), lanes] = (product[:, :W] + gam * reach).astype(bf16)
        att_ref[pl.ds(start, W), lanes] = product[:, W:] + scored[:, W:]


def layer_kernel(
    sizes, q_hbm, k_hbm, v_hbm, gate_hbm, rate_hbm, log_hbm, start_hbm, gain_hbm, w_ref, out_ref,
    q_ref, k_ref, v_ref, gate_ref, rate_ref, log_ref, start_ref, gain_ref,
    rows, cols, kk_ref, kt_ref, both_ref, maps_ref, total_ref, gam_ref, qeff_ref, att_ref,
    msg, got, shrinks, hop_out, hop_in, weights, normed, sent, came,
    load, right_s, right_r, left_s, left_r, shrink_s, shrink_r, hop_s, hop_r,
    w_own, w_s, w_r, n_s, n_r, ring_s, ring_r,
):
    nx, nz, ny = sizes
    chunks = q_ref.shape[0] // W
    seq, head = lax.axis_index("seq"), lax.axis_index("head")
    x, z = seq // nz, lax.rem(seq, nz)
    y, core = head // 2, lax.rem(head, 2)
    half = nz // 2
    step_y = 1 - 2 * core

    def seq_of(x_at, z_at):
        return lax.rem(x_at + nx, nx) * nz + lax.rem(z_at + nz, nz)

    def head_of(y_at, core_at):
        return lax.rem(y_at + ny, ny) * 2 + core_at

    next_row, last_row = (seq_of(x + 1, z), head), (seq_of(x - 1, z), head)
    sibling = (seq, head_of(y, 1 - core))
    ahead, behind = (seq, head_of(y + 1, core)), (seq, head_of(y - 1, core))
    target = (seq, head_of(y + step_y, core))
    column = [(seq_of(x, z + dz), head) for dz in range(nz)]
    above, below = column[1], column[nz - 1]

    barrier = pltpu.get_barrier_semaphore()
    greeted = (*column[1:], next_row, last_row, sibling, ahead, behind)
    for other in greeted:
        pl.semaphore_signal(barrier, inc=1, device_id=other, device_id_type=MESH)

    pairs = (
        (log_hbm, log_ref), (rate_hbm, rate_ref), (start_hbm, start_ref), (k_hbm, k_ref), (q_hbm, q_ref),
        (v_hbm, v_ref), (gate_hbm, gate_ref), (gain_hbm, gain_ref),
    )
    loads = [pltpu.make_async_copy(src, dst, load.at[n]) for n, (src, dst) in enumerate(pairs)]
    for copy in loads:
        copy.start()

    def remote(src, dst, send, recv, device):
        return pltpu.make_async_remote_copy(
            src_ref=src, dst_ref=dst, send_sem=send, recv_sem=recv, device_id=device, device_id_type=MESH
        )

    def around(t, h, upward):
        owner = lax.rem(z - t + nz, nz) if upward else lax.rem(z + t, nz)
        src = msg.at[h] if t == 0 else got.at[owner, h]
        if upward:
            return remote(src, got.at[owner, h], right_s.at[t, h], right_r.at[t, h], above)
        return remote(src, got.at[owner, h], left_s.at[t, h], left_r.at[t, h], below)

    def ways(t, h):
        return (True, False) if t < half - 1 else ((True,) if h == 0 else (False,))

    def shrink_copy(dz):
        return remote(
            shrinks.at[z], shrinks.at[z], shrink_s.at[dz], shrink_r.at[dz], column[dz]
        )

    def shrink_arrival(dz):
        at = lax.rem(z - dz + nz, nz)
        return remote(shrinks.at[at], shrinks.at[at], shrink_s.at[dz], shrink_r.at[dz], column[dz])

    def weight_copies(d):
        mine = pl.ds(pl.multiple_of((2 * d + core) * W, W), W)
        theirs = pl.ds(pl.multiple_of((2 * d + 1 - core) * W, W), W)
        own = pltpu.make_async_copy(w_ref.at[:, mine], weights.at[d, : 2 * W], w_own.at[d])
        far = remote(w_ref.at[:, theirs], weights.at[d, 2 * W :], w_s.at[d], w_r.at[d], sibling)
        return own, far

    for n in range(5):
        loads[n].wait()
    gather_vectors(q_ref, k_ref, rate_ref, log_ref, start_ref, rows, cols)
    total_ref[...] = jnp.zeros_like(total_ref)
    gam_ref[...] = jnp.ones_like(gam_ref)
    loads[5].wait()

    def work(h, i):
        shard_map_of(
            h, i, h == 0, k_ref, v_ref, rows, cols, kk_ref, kt_ref, both_ref, maps_ref, total_ref, gam_ref
        )

    def outputs(c):
        token_outputs(c, q_ref, k_ref, rows, cols, both_ref, maps_ref, gam_ref, qeff_ref, att_ref)

    def send_own(h):
        msg[h] = total_ref[h].astype(bf16)
        for upward in (True, False):
            around(0, h, upward).start()

    def pass_on(t, h):
        for upward in (True, False):
            around(t - 1, h, upward).wait_recv()
            if upward in ways(t, h):
                around(t, h, upward).start()

    def loop(count, body):
        def wrapped(i, carry):
            body(i)
            return carry

        lax.fori_loop(0, count, wrapped, 0)

    loop(chunks // GROUP, lambda i: work(0, i))
    pl.semaphore_wait(barrier, len(greeted))
    send_own(0)
    loop(chunks // GROUP, lambda i: work(1, i))
    send_own(1)
    shrinks[z] = jnp.concatenate([gam_ref[0, 0:8, :], gam_ref[1, 0:8, :]], axis=0)
    for dz in range(1, nz):
        shrink_copy(dz).start()
    for d in range(ny):
        own, far = weight_copies(d)
        own.start()
        far.start()
    for h in range(2):
        got[z, h] = msg[h]

    for t in range(1, half):
        pass_on(t, 0)
        if t == 1:
            loop(chunks // 2, outputs)
        pass_on(t, 1)
        if t == 1:
            loop(chunks // 2, lambda c: outputs(c + chunks // 2))
    for h in range(2):
        for upward in ways(half - 1, h):
            around(half - 1, h, upward).wait_recv()
    for dz in range(1, nz):
        shrink_arrival(dz).wait_recv()

    def single(at, h):
        return shrinks[at, 8 * h : 8 * h + 1, 0:1], got[at, h].astype(f32)

    zero = jnp.zeros((W, 2 * W), f32)
    whole_row, prefix = [], []
    for h in range(2):
        level = [single(at, h) for at in range(nz)]
        levels = []
        while len(level) > 1:
            levels.append(level)
            level = [compose(level[n + 1], level[n]) for n in range(0, len(level), 2)]
        whole_row.append(level[0])
        ahead_map = None
        for depth in reversed(range(len(levels))):
            here = levels[depth]
            count = lax.shift_right_logical(z, depth)
            gam, mat = jnp.ones((1, 1), f32), zero
            for n in range(0, len(here), 2):
                take = count == n + 1
                gam = jnp.where(take, here[n][0], gam)
                mat = jnp.where(take, here[n][1], mat)
            ahead_map = (gam, mat) if ahead_map is None else compose((gam, mat), ahead_map)
        prefix.append(ahead_map)

    def hop(h):
        return remote(hop_out.at[h], hop_in.at[h], hop_s.at[h], hop_r.at[h], next_row)

    @pl.when(x == 0)
    def _():
        hop_in[...] = jnp.zeros_like(hop_in)

    def enter(state, came_in):
        gam, mat = state
        return (gam * came_in.astype(f32) + dot(mat[:, :W].astype(bf16), came_in) + mat[:, W:]).astype(bf16)

    for h in range(2):
        @pl.when(x > 0)
        def _():
            hop(h).wait_recv()

        @pl.when(x < nx - 1)
        def _():
            hop_out[h] = enter(whole_row[h], hop_in[h])
            hop(h).start()

    entering = [enter(prefix[h], hop_in[h]) for h in range(2)]

    pieces = PIECES
    size = qeff_ref.shape[0] // pieces
    for n in (6, 7):
        loads[n].wait()
    gain = gain_ref[...]

    def normed_copy(p):
        return remote(normed.at[0, p], normed.at[1, p], n_s.at[p], n_r.at[p], sibling)

    def make_normed(p):
        here = slice(p * size, (p + 1) * size)
        for h in range(2):
            lanes = slice(h * W, (h + 1) * W)
            attended = att_ref[here, lanes] + dot(qeff_ref[here, lanes], entering[h])
            scale = lax.rsqrt(jnp.mean(attended * attended, axis=1, keepdims=True) + 1e-6)
            gate = gate_ref[here, lanes].astype(f32)
            normed[0, p, :, lanes] = (attended * scale * gain * (gate / (1.0 + jnp.exp(-gate)))).astype(bf16)

    def partial(p, d):
        return dot(normed[0, p], weights[d, : 2 * W]) + dot(normed[1, p], weights[d, 2 * W :])

    def ring(s, p):
        return remote(sent.at[s, p], came.at[s, p], ring_s.at[s, p], ring_r.at[s, p], target)

    def block_of(s):
        return lax.rem(y - step_y * (s + 1) + 2 * ny, ny)

    def first_step(p):
        normed_copy(p).wait_recv()
        sent[0, p] = partial(p, block_of(0)).astype(bf16)
        ring(0, p).start()

    for p in range(pieces):
        make_normed(p)
        normed_copy(p).start()
        if p == 0:
            for d in range(ny):
                own, far = weight_copies(d)
                own.wait()
                far.wait_recv()
        if p > 0:
            first_step(p - 1)
    first_step(pieces - 1)

    def step(s):
        d = block_of(s)
        for p in range(pieces):
            mine = partial(p, d)
            ring(s - 1, p).wait_recv()
            sent[s, p] = (mine + came[s - 1, p].astype(f32)).astype(bf16)
            ring(s, p).start()

    loop(ny - 2, lambda s: step(s + 1))
    for p in range(pieces):
        mine = partial(p, y)
        ring(ny - 2, p).wait_recv()
        out_ref[p * size : (p + 1) * size, :] = (mine + came[ny - 2, p].astype(f32)).astype(bf16)

    for t in range(half):
        for h in range(2):
            for upward in ways(t, h):
                around(t, h, upward).wait_send()
    for dz in range(1, nz):
        shrink_copy(dz).wait_send()
    for d in range(ny):
        weight_copies(d)[1].wait_send()
    for h in range(2):
        @pl.when(x < nx - 1)
        def _():
            hop(h).wait_send()
    for p in range(pieces):
        normed_copy(p).wait_send()

    def drain(s):
        for p in range(pieces):
            ring(s, p).wait_send()

    loop(ny - 1, drain)


def layer(sizes, *arrays):
    nx, nz, ny = sizes
    tokens = arrays[0].shape[0]
    chunks = tokens // W
    half = nz // 2
    size = tokens // PIECES
    dma = pltpu.SemaphoreType.DMA

    def kernel(*refs):
        layer_kernel(sizes, *refs)

    return pl.pallas_call(
        kernel,
        out_shape=jax.ShapeDtypeStruct((tokens, W), bf16),
        in_specs=[pl.BlockSpec(memory_space=pltpu.MemorySpace.HBM)] * 9,
        out_specs=pl.BlockSpec(memory_space=pltpu.VMEM),
        scratch_shapes=[
            *[pltpu.VMEM(a.shape, a.dtype) for a in arrays[:8]],
            pltpu.VMEM((8 * chunks, W), f32),
            pltpu.VMEM((chunks, W, 8), f32),
            pltpu.VMEM((chunks, W, W), f32),
            pltpu.VMEM((chunks, W, W), bf16),
            pltpu.VMEM((chunks, 2, W, 2 * W), bf16),
            pltpu.VMEM((chunks, 2, W, 2 * W), bf16),
            pltpu.VMEM((2, W, 2 * W), f32),
            pltpu.VMEM((2, 8 + chunks, W), f32),
            pltpu.VMEM((tokens, 2 * W), bf16),
            pltpu.VMEM((tokens, 2 * W), f32),
            pltpu.VMEM((2, W, 2 * W), bf16),
            pltpu.VMEM((nz, 2, W, 2 * W), bf16),
            pltpu.VMEM((nz, 16, W), f32),
            pltpu.VMEM((2, W, W), bf16),
            pltpu.VMEM((2, W, W), bf16),
            pltpu.VMEM((ny, 4 * W, W), bf16),
            pltpu.VMEM((2, PIECES, size, 2 * W), bf16),
            pltpu.VMEM((ny - 1, PIECES, size, W), bf16),
            pltpu.VMEM((ny - 1, PIECES, size, W), bf16),
            dma((8,)),
            dma((half, 2)), dma((half, 2)), dma((half, 2)), dma((half, 2)),
            dma((nz,)), dma((nz,)),
            dma((2,)), dma((2,)),
            dma((ny,)), dma((ny,)), dma((ny,)),
            dma((PIECES,)), dma((PIECES,)),
            dma((ny - 1, PIECES)), dma((ny - 1, PIECES)),
        ],
        compiler_params=pltpu.CompilerParams(
            collective_id=0, has_side_effects=True, vmem_limit_bytes=56 << 20
        ),
    )(*arrays)


def build(mesh, sizes):
    def local(queries, keys, values, gate, rates, logs, starts, gain, weight):
        return layer(
            sizes, queries, keys, values, gate, rates, logs, starts.reshape(-1, W), gain.reshape(1, W), weight
        )

    both = P("seq", "head")
    placed = (both, both, both, both, P("head", "seq"), P("head", "seq"), P("seq"), P(), P("head", None))
    return jax.shard_map(local, mesh=mesh, in_specs=placed, out_specs=both, check_vma=False)


def solution(mesh):
    return build(mesh, (NX, NZ, NY))
```

time: 94.6 us -> 79.1 us (0.84)
  Pallas kernels: 86.7 us -> 77.3 us
  local copies, waits for them, and re-layouts: 7.5 us -> 1.67 us
    pallas_call x2 -> x1, Pallas kernels: 86.7 us -> 77.3 us  [layer(): pl.pallas_call(kernel, out_shape=jax.ShapeDtypeStruct((tokens, W), bf16),...]
    unnamed x19 -> x1, local copies, waits for them, and re-layouts: 7.5 us -> 1.67 us
where the time goes in v2:
time: 79.1 us; the launch traced here: 78.9 us
  Pallas kernels  77.3 us (98%)
  local copies, waits for them, and re-layouts  1.67 us (2%)
    pallas_call x1, Pallas kernels, layer(): pl.pallas_call(kernel, out_shape=jax.ShapeDtypeStruct((tokens, W), bf16),...  77.3 us
    unnamed x1, local copies, waits for them, and re-layouts  1.67 us

profile of v2, /device:TPU:6, one launch (start us, length us, event | category | flops | bytes accessed | tf_op | source)
XLA Modules:
  0.0 78.9 jit_solution(303113855159434420)
XLA Ops:
  0.0 77.3 %shard_map.91 = bf16[1024,128]{1,0:T(8,128)(2,1)} custom-call(bf16[1024,128]{1,0:T(8,128)(2,1)} %refs_0_.1, bf16[1024,128]{1,0:T(8,128)(2,1)} %refs_1_.1, bf16[1024,256]{1,0:T(8,128)(2,1)} %refs_2_.1, bf16[1024,256]{1,0:T(8,128)(2,1)} %refs_3_.1, f32[2,1024]{1,0:T(2,128)} %refs_4_.1, f32[2,1024]{1,0:T(2,128)} %refs_5_.1, s32[8,128]{1,0:T(8,128)} %bitcast.2, ...), custom_call_target="tpu_custom_call" | custom-call | tf_op jit(solution)/shard_map/pallas_call | solution.py:450
  77.3 1.7 %copy.11 = bf16[1024,128]{1,0:T(8,128)(2,1)} copy(bf16[1024,128]{1,0:T(8,128)(2,1)} %shard_map.91) | data formatting | bytes 524288

commit v3 on v2

--- a/solution.py
+++ b/solution.py
@@ -9,6 +9,8 @@
 NX, NZ, NY = 4, 8, 8
 PIECES = 4
 GROUP = 4
+PARTS = 4
+PART_ROWS = 2 * W // PARTS
 f32, bf16 = jnp.float32, jnp.bfloat16
 MESH = pl.DeviceIdType.MESH
 
@@ -32,7 +34,7 @@
     return lax.broadcasted_iota(jnp.int32, (W, W), 0), lax.broadcasted_iota(jnp.int32, (W, W), 1)
 
 
-def gather_vectors(q_ref, k_ref, rate_ref, log_ref, start_ref, rows, cols):
+def gather_vectors(k_ref, rate_ref, log_ref, start_ref, rows, cols):
     chunks = k_ref.shape[0] // W
     row, col = iotas()
     eye = row == col
@@ -53,11 +55,9 @@
     for c in range(chunks):
         here = slice(c * W, (c + 1) * W)
         kf = k_ref[here, :].astype(f32)
-        qf = q_ref[here, :].astype(f32)
         rk_c = lax.rsqrt(jnp.sum(kf * kf, axis=1, keepdims=True) + 1e-6)
-        rq_c = lax.rsqrt(jnp.sum(qf * qf, axis=1, keepdims=True) + 1e-6)
         rows[8 * c + 5 : 8 * c + 6, :] = jnp.sum(jnp.where(eye, rk_c, 0.0), axis=0, keepdims=True)
-        cols[c] = jnp.where(lane == 5, rk_c, jnp.where(lane == 6, rq_c, turned[:, 8 * c : 8 * c + 8]))
+        cols[c] = jnp.where(lane == 5, rk_c, turned[:, 8 * c : 8 * c + 8])
 
 
 def chunk_at(ref, c):
@@ -74,117 +74,130 @@
     return jnp.exp(jnp.where(same, vec_c[:, h : h + 1] - vec_r[h : h + 1], -1e9))
 
 
-def odd_rows(values, size):
-    return jnp.concatenate([values[at : at + size] for at in range(size, W, 2 * size)], axis=0)
+def twin(pair):
+    zero = jnp.zeros((pair.shape[0], W), pair.dtype)
+    return jnp.concatenate(
+        [jnp.concatenate([pair[:, :W], zero], axis=1), jnp.concatenate([zero, pair[:, W:]], axis=1)], axis=0
+    )
 
 
 def refine(inverse, coupling, size):
-    if size < 8:
-        row, col = iotas()
-        block = (row // (2 * size) == col // (2 * size)) & (row // size > col // size)
-        inv_b = inverse.astype(bf16)
-        part = dot(jnp.where(block, coupling, 0.0).astype(bf16), inv_b)
-        return inverse - dot(inv_b, part.astype(bf16))
-    row = lax.broadcasted_iota(jnp.int32, (W // 2, W), 0)
-    col = lax.broadcasted_iota(jnp.int32, (W // 2, W), 1)
-    block = 2 * (row // size) == col // size
-    left = jnp.where(block, odd_rows(coupling, size), 0.0).astype(bf16)
-    part = dot(left, inverse.astype(bf16))
-    zeros = jnp.zeros((size, W), f32)
-    spread = []
-    for at in range(0, W // 2, size):
-        spread += [zeros, part[at : at + size]]
-    odd = odd_rows(inverse, size)
-    odd = odd - dot(odd.astype(bf16), jnp.concatenate(spread, axis=0).astype(bf16))
-    mixed = []
-    for at in range(0, W // 2, size):
-        mixed += [inverse[2 * at : 2 * at + size], odd[at : at + size]]
-    return jnp.concatenate(mixed, axis=0)
-
-
-def shard_map_of(h, i, first, k_ref, v_ref, rows, cols, kk_ref, kt_ref, both_ref, maps_ref, total_ref, gam_ref):
-    row, col = iotas()
+    row, col = pair_iotas()
+    block = (row // (4 * size) == col // (4 * size)) & (row // size > col // size)
+    inv_b = inverse.astype(bf16)
+    n = dot(inv_b, twin(jnp.where(block, coupling, 0.0).astype(bf16))).astype(bf16)
+    squared = dot(n, twin(n)).astype(bf16)
+    once = inverse - dot(n, twin(inv_b))
+    return once + dot(squared, twin(once.astype(bf16)))
+
+
+def pair_iotas():
+    row = lax.broadcasted_iota(jnp.int32, (W, 2 * W), 0)
+    col = lax.broadcasted_iota(jnp.int32, (W, 2 * W), 1)
+    return row, lax.rem(col, W)
+
+
+def shard_maps(i, group, k_ref, v_ref, rows, cols, both_ref, maps_ref, total_ref, gam_ref):
+    row, col = pair_iotas()
+
+    def side(parts):
+        return jnp.concatenate(parts, axis=1)
+
     found = []
-    for j in range(GROUP):
-        c = GROUP * i + j
+    for j in range(group):
+        c = group * i + j
         vec_r, vec_c = vectors_at(rows, cols, c)
-        if first:
-            kc = chunk_at(k_ref, c)
-            kk = dot_t(kc, kc) * vec_c[:, 5:6] * vec_r[5:6]
-            kk_ref[c] = kk
-            kt_ref[c] = jnp.transpose(kc.astype(f32)).astype(bf16)
-        else:
-            kk = kk_ref[c]
-        coupling = vec_c[:, 3 + h : 4 + h] * kk * decay_of(vec_r, vec_c, h)
+        kc = chunk_at(k_ref, c)
+        kk = dot_t(kc, kc) * vec_c[:, 5:6] * vec_r[5:6]
+        coupling = side([vec_c[:, 3 + h : 4 + h] * kk * decay_of(vec_r, vec_c, h) for h in range(2)])
         near = jnp.where((row // 2 == col // 2) & (row >= col), -coupling, 0.0)
         found.append([coupling, jnp.where(row == col, 1.0, near)])
-    size = 2
-    while size < W:
-        for j in range(GROUP):
-            found[j][1] = refine(found[j][1], found[j][0], size)
-        size *= 2
-    moves = []
-    for j in range(GROUP):
-        c = GROUP * i + j
+    for size in (2, 8, 32):
+        for entry in found:
+            entry[1] = refine(entry[1], entry[0], size)
+    moves = {}
+    for j in range(group):
+        c = group * i + j
+        vec_r, vec_c = vectors_at(rows, cols, c)
+        kc = chunk_at(k_ref, c)
+        k_turned = jnp.transpose(kc.astype(f32)).astype(bf16)
         inverse = found[j][1]
+        rk_r = vec_r[5:6]
+        reset_r, reset_c = vec_r[2:3], vec_c[:, 2:3]
+        reset_last = reset_r[:, W - 1 : W]
+        rates = [vec_r[3 + h : 4 + h] for h in range(2)]
+        heads = [jnp.where(reset_r == 0.0, jnp.exp(vec_r[h : h + 1]), 0.0) for h in range(2)]
+        scale = side([rates[h] * heads[h] * rk_r for h in range(2)])
+        erase = dot((inverse * scale).astype(bf16), twin(side([kc, kc])))
+        write = dot((inverse * side(rates)).astype(bf16), twin(chunk_at(v_ref, c)))
+        for h in range(2):
+            lanes = slice(h * W, (h + 1) * W)
+            g_c = vec_c[:, h : h + 1]
+            g_last = vec_r[h : h + 1, W - 1 : W]
+            tail_c = jnp.where(reset_c == reset_last, jnp.exp(g_last - g_c), 0.0)
+            whole = jnp.where(reset_last == 0.0, jnp.exp(g_last), 0.0)
+            both = side([erase[:, lanes], write[:, lanes]])
+            both_ref[c, h] = both.astype(bf16)
+            moves[j, h] = (whole, dot(k_turned, (both * (tail_c * vec_c[:, 5:6])).astype(bf16)))
+    totals = [total_ref[h] for h in range(2)]
+    gams = [gam_ref[h, 0:1, :] for h in range(2)]
+    for j in range(group):
+        c = group * i + j
+        for h in range(2):
+            whole, moved = moves[j, h]
+            total, gam = totals[h], gams[h]
+            total_b = total.astype(bf16)
+            maps_ref[c, h] = total_b
+            gam_ref[h, pl.ds(8 + c, 1), :] = gam
+            totals[h] = (
+                whole * total
+                - dot(moved[:, :W].astype(bf16), total_b)
+                + jnp.concatenate([-gam * moved[:, :W], moved[:, W:]], axis=1)
+            )
+            gams[h] = gam * whole
+    for h in range(2):
+        total_ref[h] = totals[h]
+        gam_ref[h, 0:1, :] = gams[h]
+
+
+def token_outputs(first, count, q_ref, k_ref, rows, cols, both_ref, maps_ref, gam_ref, qeff_ref, att_ref):
+    scores = []
+    for c in range(first, first + count):
         vec_r, vec_c = vectors_at(rows, cols, c)
-        g_r, g_c, b_r, rk_r = vec_r[h : h + 1], vec_c[:, h : h + 1], vec_r[3 + h : 4 + h], vec_r[5:6]
-        reset_r, reset_c = vec_r[2:3], vec_c[:, 2:3]
-        g_last, reset_last = g_r[:, W - 1 : W], reset_r[:, W - 1 : W]
-        head_r = jnp.where(reset_r == 0.0, jnp.exp(g_r), 0.0)
-        tail_c = jnp.where(reset_c == reset_last, jnp.exp(g_last - g_c), 0.0)
-        whole = jnp.where(reset_last == 0.0, jnp.exp(g_last), 0.0)
-        erase = dot((inverse * (b_r * head_r * rk_r)).astype(bf16), chunk_at(k_ref, c))
-        values = v_ref[pl.ds(pl.multiple_of(c * W, W), W), h * W : (h + 1) * W]
-        write = dot((inverse * b_r).astype(bf16), values)
-        both = jnp.concatenate([erase, write], axis=1)
-        both_ref[c, h] = both.astype(bf16)
-        moves.append((whole, dot(kt_ref[c], (both * (tail_c * vec_c[:, 5:6])).astype(bf16))))
-    total, gam = total_ref[h], gam_ref[h, 0:1, :]
-    for j in range(GROUP):
-        c = GROUP * i + j
-        whole, moved = moves[j]
-        total_b = total.astype(bf16)
-        maps_ref[c, h] = total_b
-        gam_ref[h, pl.ds(8 + c, 1), :] = gam
-        total = (
-            whole * total
-            - dot(moved[:, :W].astype(bf16), total_b)
-            + jnp.concatenate([-gam * moved[:, :W], moved[:, W:]], axis=1)
-        )
-        gam = gam * whole
-    total_ref[h] = total
-    gam_ref[h, 0:1, :] = gam
-
-
-def token_outputs(c, q_ref, k_ref, rows, cols, both_ref, maps_ref, gam_ref, qeff_ref, att_ref):
-    start = pl.multiple_of(c * W, W)
-    vec_r, vec_c = vectors_at(rows, cols, c)
-    qc = chunk_at(q_ref, c)
-    qk = dot_t(qc, chunk_at(k_ref, c)) * vec_c[:, 6:7] * vec_r[5:6]
-    for h in range(2):
-        both = both_ref[c, h]
-        g_c, reset_c = vec_c[:, h : h + 1], vec_c[:, 2:3]
-        head_c = jnp.where(reset_c == 0.0, jnp.exp(g_c), 0.0)
-        scored = dot((qk * decay_of(vec_r, vec_c, h)).astype(bf16), both)
-        reach = qc.astype(f32) * (head_c * vec_c[:, 6:7]) - scored[:, :W]
-        product = dot(reach.astype(bf16), maps_ref[c, h])
-        lanes = slice(h * W, (h + 1) * W)
-        gam = gam_ref[h, pl.ds(8 + c, 1), :]
-        qeff_ref[pl.ds(start, W), lanes] = (product[:, :W] + gam * reach).astype(bf16)
-        att_ref[pl.ds(start, W), lanes] = product[:, W:] + scored[:, W:]
+        qc = chunk_at(q_ref, c)
+        qf = qc.astype(f32)
+        rq_c = lax.rsqrt(jnp.sum(qf * qf, axis=1, keepdims=True) + 1e-6)
+        qk = dot_t(qc, chunk_at(k_ref, c)) * rq_c * vec_r[5:6]
+        scores.append((qf * rq_c, [(qk * decay_of(vec_r, vec_c, h)).astype(bf16) for h in range(2)]))
+    scored = [
+        [dot(scores[c - first][1][h], both_ref[c, h]) for h in range(2)] for c in range(first, first + count)
+    ]
+    for c in range(first, first + count):
+        here = slice(c * W, (c + 1) * W)
+        vec_r, vec_c = vectors_at(rows, cols, c)
+        for h in range(2):
+            g_c, reset_c = vec_c[:, h : h + 1], vec_c[:, 2:3]
+            head_c = jnp.where(reset_c == 0.0, jnp.exp(g_c), 0.0)
+            mine = scored[c - first][h]
+            reach = scores[c - first][0] * head_c - mine[:, :W]
+            product = dot(reach.astype(bf16), maps_ref[c, h])
+            lanes = slice(h * W, (h + 1) * W)
+            gam = gam_ref[h, 8 + c : 9 + c, :]
+            qeff_ref[here, lanes] = (product[:, :W] + gam * reach).astype(bf16)
+            att_ref[here, lanes] = product[:, W:] + mine[:, W:]
 
 
 def layer_kernel(
     sizes, q_hbm, k_hbm, v_hbm, gate_hbm, rate_hbm, log_hbm, start_hbm, gain_hbm, w_ref, out_ref,
     q_ref, k_ref, v_ref, gate_ref, rate_ref, log_ref, start_ref, gain_ref,
-    rows, cols, kk_ref, kt_ref, both_ref, maps_ref, total_ref, gam_ref, qeff_ref, att_ref,
+    rows, cols, both_ref, maps_ref, total_ref, gam_ref, qeff_ref, att_ref,
     msg, got, shrinks, hop_out, hop_in, weights, normed, sent, came,
     load, right_s, right_r, left_s, left_r, shrink_s, shrink_r, hop_s, hop_r,
     w_own, w_s, w_r, n_s, n_r, ring_s, ring_r,
 ):
     nx, nz, ny = sizes
     chunks = q_ref.shape[0] // W
+    group = min(GROUP, chunks)
     seq, head = lax.axis_index("seq"), lax.axis_index("head")
     x, z = seq // nz, lax.rem(seq, nz)
     y, core = head // 2, lax.rem(head, 2)
@@ -230,7 +243,7 @@
         return remote(src, got.at[owner, h], left_s.at[t, h], left_r.at[t, h], below)
 
     def ways(t, h):
-        return (True, False) if t < half - 1 else ((True,) if h == 0 else (False,))
+        return (True, False) if t < half - 1 else ((True,) if h < PARTS // 2 else (False,))
 
     def shrink_copy(dz):
         return remote(
@@ -250,23 +263,16 @@
 
     for n in range(5):
         loads[n].wait()
-    gather_vectors(q_ref, k_ref, rate_ref, log_ref, start_ref, rows, cols)
+    gather_vectors(k_ref, rate_ref, log_ref, start_ref, rows, cols)
     total_ref[...] = jnp.zeros_like(total_ref)
     gam_ref[...] = jnp.ones_like(gam_ref)
     loads[5].wait()
 
-    def work(h, i):
-        shard_map_of(
-            h, i, h == 0, k_ref, v_ref, rows, cols, kk_ref, kt_ref, both_ref, maps_ref, total_ref, gam_ref
-        )
-
-    def outputs(c):
-        token_outputs(c, q_ref, k_ref, rows, cols, both_ref, maps_ref, gam_ref, qeff_ref, att_ref)
-
-    def send_own(h):
-        msg[h] = total_ref[h].astype(bf16)
-        for upward in (True, False):
-            around(0, h, upward).start()
+    def work(i):
+        shard_maps(i, group, k_ref, v_ref, rows, cols, both_ref, maps_ref, total_ref, gam_ref)
+
+    def outputs(first, count):
+        token_outputs(first, count, q_ref, k_ref, rows, cols, both_ref, maps_ref, gam_ref, qeff_ref, att_ref)
 
     def pass_on(t, h):
         for upward in (True, False):
@@ -281,11 +287,13 @@
 
         lax.fori_loop(0, count, wrapped, 0)
 
-    loop(chunks // GROUP, lambda i: work(0, i))
+    loop(chunks // group, work)
     pl.semaphore_wait(barrier, len(greeted))
-    send_own(0)
-    loop(chunks // GROUP, lambda i: work(1, i))
-    send_own(1)
+    for part in range(PARTS):
+        h, rows_at = part // (PARTS // 2), part % (PARTS // 2) * PART_ROWS
+        msg[part] = total_ref[h, rows_at : rows_at + PART_ROWS].astype(bf16)
+        for upward in (True, False):
+            around(0, part, upward).start()
     shrinks[z] = jnp.concatenate([gam_ref[0, 0:8, :], gam_ref[1, 0:8, :]], axis=0)
     for dz in range(1, nz):
         shrink_copy(dz).start()
@@ -293,24 +301,22 @@
         own, far = weight_copies(d)
         own.start()
         far.start()
-    for h in range(2):
-        got[z, h] = msg[h]
-
+    got[z] = msg[...]
+
+    shares = [chunks * n // (half - 1) for n in range(half)] if half > 1 else [0, chunks]
     for t in range(1, half):
-        pass_on(t, 0)
-        if t == 1:
-            loop(chunks // 2, outputs)
-        pass_on(t, 1)
-        if t == 1:
-            loop(chunks // 2, lambda c: outputs(c + chunks // 2))
-    for h in range(2):
-        for upward in ways(half - 1, h):
-            around(half - 1, h, upward).wait_recv()
+        outputs(shares[t - 1], shares[t] - shares[t - 1])
+        for part in range(PARTS):
+            pass_on(t, part)
+    for part in range(PARTS):
+        for upward in ways(half - 1, part):
+            around(half - 1, part, upward).wait_recv()
     for dz in range(1, nz):
         shrink_arrival(dz).wait_recv()
 
     def single(at, h):
-        return shrinks[at, 8 * h : 8 * h + 1, 0:1], got[at, h].astype(f32)
+        pair = [got[at, n] for n in range(h * PARTS // 2, (h + 1) * PARTS // 2)]
+        return shrinks[at, 8 * h : 8 * h + 1, 0:1], jnp.concatenate(pair, axis=0).astype(f32)
 
     zero = jnp.zeros((W, 2 * W), f32)
     whole_row, prefix = [], []
@@ -415,9 +421,9 @@
         out_ref[p * size : (p + 1) * size, :] = (mine + came[ny - 2, p].astype(f32)).astype(bf16)
 
     for t in range(half):
-        for h in range(2):
-            for upward in ways(t, h):
-                around(t, h, upward).wait_send()
+        for part in range(PARTS):
+            for upward in ways(t, part):
+                around(t, part, upward).wait_send()
     for dz in range(1, nz):
         shrink_copy(dz).wait_send()
     for d in range(ny):
@@ -456,16 +462,14 @@
             *[pltpu.VMEM(a.shape, a.dtype) for a in arrays[:8]],
             pltpu.VMEM((8 * chunks, W), f32),
             pltpu.VMEM((chunks, W, 8), f32),
-            pltpu.VMEM((chunks, W, W), f32),
-            pltpu.VMEM((chunks, W, W), bf16),
             pltpu.VMEM((chunks, 2, W, 2 * W), bf16),
             pltpu.VMEM((chunks, 2, W, 2 * W), bf16),
             pltpu.VMEM((2, W, 2 * W), f32),
             pltpu.VMEM((2, 8 + chunks, W), f32),
             pltpu.VMEM((tokens, 2 * W), bf16),
             pltpu.VMEM((tokens, 2 * W), f32),
-            pltpu.VMEM((2, W, 2 * W), bf16),
-            pltpu.VMEM((nz, 2, W, 2 * W), bf16),
+            pltpu.VMEM((PARTS, PART_ROWS, 2 * W), bf16),
+            pltpu.VMEM((nz, PARTS, PART_ROWS, 2 * W), bf16),
             pltpu.VMEM((nz, 16, W), f32),
             pltpu.VMEM((2, W, W), bf16),
             pltpu.VMEM((2, W, W), bf16),
@@ -474,7 +478,7 @@
             pltpu.VMEM((ny - 1, PIECES, size, W), bf16),
             pltpu.VMEM((ny - 1, PIECES, size, W), bf16),
             dma((8,)),
-            dma((half, 2)), dma((half, 2)), dma((half, 2)), dma((half, 2)),
+            dma((half, PARTS)), dma((half, PARTS)), dma((half, PARTS)), dma((half, PARTS)),
             dma((nz,)), dma((nz,)),
             dma((2,)), dma((2,)),
             dma((ny,)), dma((ny,)), dma((ny,)),

time: 79.1 us -> 76.4 us (0.966)
  Pallas kernels: 77.3 us -> 74.5 us
    pallas_call x1, Pallas kernels: 77.3 us -> 74.5 us  [layer(): pl.pallas_call(kernel, out_shape=jax.ShapeDtypeStruct((tokens, W), bf16),...]
where the time goes in v3:
time: 76.4 us; the launch traced here: 76.2 us
  Pallas kernels  74.5 us (98%)
  local copies, waits for them, and re-layouts  1.67 us (2%)
    pallas_call x1, Pallas kernels, layer(): pl.pallas_call(kernel, out_shape=jax.ShapeDtypeStruct((tokens, W), bf16),...  74.5 us
    unnamed x1, local copies, waits for them, and re-layouts  1.67 us

profile of v3, /device:TPU:6, one launch (start us, length us, event | category | flops | bytes accessed | tf_op | source)
XLA Modules:
  0.0 76.2 jit_solution(14375439978405367465)
XLA Ops:
  0.0 74.5 %shard_map.91 = bf16[1024,128]{1,0:T(8,128)(2,1)} custom-call(bf16[1024,128]{1,0:T(8,128)(2,1)} %refs_0_.1, bf16[1024,128]{1,0:T(8,128)(2,1)} %refs_1_.1, bf16[1024,256]{1,0:T(8,128)(2,1)} %refs_2_.1, bf16[1024,256]{1,0:T(8,128)(2,1)} %refs_3_.1, f32[2,1024]{1,0:T(2,128)} %refs_4_.1, f32[2,1024]{1,0:T(2,128)} %refs_5_.1, s32[8,128]{1,0:T(8,128)} %bitcast.2, ...), custom_call_target="tpu_custom_call" | custom-call | tf_op jit(solution)/shard_map/pallas_call | solution.py:456
  74.6 1.7 %copy.11 = bf16[1024,128]{1,0:T(8,128)(2,1)} copy(bf16[1024,128]{1,0:T(8,128)(2,1)} %shard_map.91) | data formatting | bytes 524288

commit v4 on v3

--- a/solution.py
+++ b/solution.py
@@ -9,7 +9,7 @@
 NX, NZ, NY = 4, 8, 8
 PIECES = 4
 GROUP = 4
-PARTS = 4
+PARTS = 2
 PART_ROWS = 2 * W // PARTS
 f32, bf16 = jnp.float32, jnp.bfloat16
 MESH = pl.DeviceIdType.MESH
@@ -61,11 +61,12 @@
 
 
 def chunk_at(ref, c):
-    return ref[pl.ds(pl.multiple_of(c * W, W), W), :]
+    return ref[c * W : (c + 1) * W, :] if isinstance(c, int) else ref[pl.ds(pl.multiple_of(c * W, W), W), :]
 
 
 def vectors_at(rows, cols, c):
-    return rows[pl.ds(pl.multiple_of(c * 8, 8), 8), :], cols[c]
+    at = slice(8 * c, 8 * c + 8) if isinstance(c, int) else pl.ds(pl.multiple_of(c * 8, 8), 8)
+    return rows[at, :], cols[c]
 
 
 def decay_of(vec_r, vec_c, h):
@@ -191,7 +192,7 @@
     sizes, q_hbm, k_hbm, v_hbm, gate_hbm, rate_hbm, log_hbm, start_hbm, gain_hbm, w_ref, out_ref,
     q_ref, k_ref, v_ref, gate_ref, rate_ref, log_ref, start_ref, gain_ref,
     rows, cols, both_ref, maps_ref, total_ref, gam_ref, qeff_ref, att_ref,
-    msg, got, shrinks, hop_out, hop_in, weights, normed, sent, came,
+    msg, got, shrinks, hop_out, hop_in, map_out, map_in, lead, weights, normed, sent, came,
     load, right_s, right_r, left_s, left_r, shrink_s, shrink_r, hop_s, hop_r,
     w_own, w_s, w_r, n_s, n_r, ring_s, ring_r,
 ):
@@ -211,6 +212,7 @@
         return lax.rem(y_at + ny, ny) * 2 + core_at
 
     next_row, last_row = (seq_of(x + 1, z), head), (seq_of(x - 1, z), head)
+    third_row = (seq_of(x + 2, z), head)
     sibling = (seq, head_of(y, 1 - core))
     ahead, behind = (seq, head_of(y + 1, core)), (seq, head_of(y - 1, core))
     target = (seq, head_of(y + step_y, core))
@@ -218,7 +220,7 @@
     above, below = column[1], column[nz - 1]
 
     barrier = pltpu.get_barrier_semaphore()
-    greeted = (*column[1:], next_row, last_row, sibling, ahead, behind)
+    greeted = (*column[1:], next_row, last_row, third_row, sibling, ahead, behind)
     for other in greeted:
         pl.semaphore_signal(barrier, inc=1, device_id=other, device_id_type=MESH)
 
@@ -246,20 +248,21 @@
         return (True, False) if t < half - 1 else ((True,) if h < PARTS // 2 else (False,))
 
     def shrink_copy(dz):
-        return remote(
-            shrinks.at[z], shrinks.at[z], shrink_s.at[dz], shrink_r.at[dz], column[dz]
-        )
-
-    def shrink_arrival(dz):
-        at = lax.rem(z - dz + nz, nz)
-        return remote(shrinks.at[at], shrinks.at[at], shrink_s.at[dz], shrink_r.at[dz], column[dz])
+        return remote(shrinks.at[z], shrinks.at[z], shrink_s, shrink_r, column[dz])
+
+    def all_shrinks():
+        return remote(shrinks.at[: nz - 1], shrinks.at[: nz - 1], shrink_s, shrink_r, column[1])
 
     def weight_copies(d):
         mine = pl.ds(pl.multiple_of((2 * d + core) * W, W), W)
         theirs = pl.ds(pl.multiple_of((2 * d + 1 - core) * W, W), W)
-        own = pltpu.make_async_copy(w_ref.at[:, mine], weights.at[d, : 2 * W], w_own.at[d])
-        far = remote(w_ref.at[:, theirs], weights.at[d, 2 * W :], w_s.at[d], w_r.at[d], sibling)
+        own = pltpu.make_async_copy(w_ref.at[:, mine], weights.at[d, : 2 * W], w_own)
+        far = remote(w_ref.at[:, theirs], weights.at[d, 2 * W :], w_s, w_r, sibling)
         return own, far
+
+    def all_weights():
+        near, rest = weights.at[:, : 2 * W], weights.at[:, 2 * W :]
+        return pltpu.make_async_copy(near, near, w_own), remote(rest, rest, w_s, w_r, sibling)
 
     for n in range(5):
         loads[n].wait()
@@ -287,13 +290,19 @@
 
         lax.fori_loop(0, count, wrapped, 0)
 
-    loop(chunks // group, work)
+    if chunks == group:
+        work(0)
+    else:
+        loop(chunks // group, work)
     pl.semaphore_wait(barrier, len(greeted))
-    for part in range(PARTS):
-        h, rows_at = part // (PARTS // 2), part % (PARTS // 2) * PART_ROWS
-        msg[part] = total_ref[h, rows_at : rows_at + PART_ROWS].astype(bf16)
-        for upward in (True, False):
-            around(0, part, upward).start()
+    def send_own(h):
+        for n in range(PARTS // 2):
+            part = h * PARTS // 2 + n
+            msg[part] = total_ref[h, n * PART_ROWS : (n + 1) * PART_ROWS].astype(bf16)
+            for upward in (True, False):
+                around(0, part, upward).start()
+
+    send_own(0)
     shrinks[z] = jnp.concatenate([gam_ref[0, 0:8, :], gam_ref[1, 0:8, :]], axis=0)
     for dz in range(1, nz):
         shrink_copy(dz).start()
@@ -301,18 +310,23 @@
         own, far = weight_copies(d)
         own.start()
         far.start()
+    shares = [chunks * n // half for n in range(half + 1)]
+    outputs(0, shares[1])
+    for part in range(PARTS // 2):
+        for upward in ways(0, part):
+            around(0, part, upward).wait_send()
+    send_own(1)
     got[z] = msg[...]
 
-    shares = [chunks * n // (half - 1) for n in range(half)] if half > 1 else [0, chunks]
     for t in range(1, half):
-        outputs(shares[t - 1], shares[t] - shares[t - 1])
         for part in range(PARTS):
             pass_on(t, part)
+            if part == PARTS // 2 - 1:
+                outputs(shares[t], shares[t + 1] - shares[t])
     for part in range(PARTS):
         for upward in ways(half - 1, part):
             around(half - 1, part, upward).wait_recv()
-    for dz in range(1, nz):
-        shrink_arrival(dz).wait_recv()
+    all_shrinks().wait_recv()
 
     def single(at, h):
         pair = [got[at, n] for n in range(h * PARTS // 2, (h + 1) * PARTS // 2)]
@@ -339,28 +353,79 @@
             ahead_map = (gam, mat) if ahead_map is None else compose((gam, mat), ahead_map)
         prefix.append(ahead_map)
 
-    def hop(h):
+    def enter(state, came_in):
+        gam, mat = state
+        return gam * came_in.astype(f32) + dot(mat[:, :W].astype(bf16), came_in) + mat[:, W:]
+
+    def first_hop(h):
         return remote(hop_out.at[h], hop_in.at[h], hop_s.at[h], hop_r.at[h], next_row)
+
+    def map_hop(h):
+        return remote(map_out.at[h], map_in.at[h], hop_s.at[2 + h], hop_r.at[2 + h], next_row)
+
+    def second_hop(h, far):
+        n = 4 + 2 * far + h
+        return remote(hop_out.at[h], hop_in.at[h], hop_s.at[n], hop_r.at[n], third_row if far else next_row)
+
+    if nx not in (2, 4):
+        raise ValueError("rows")
 
     @pl.when(x == 0)
     def _():
         hop_in[...] = jnp.zeros_like(hop_in)
-
-    def enter(state, came_in):
-        gam, mat = state
-        return (gam * came_in.astype(f32) + dot(mat[:, :W].astype(bf16), came_in) + mat[:, W:]).astype(bf16)
-
-    for h in range(2):
-        @pl.when(x > 0)
+        for h in range(2):
+            hop_out[h] = whole_row[h][1][:, W:].astype(bf16)
+            first_hop(h).start()
+
+    @pl.when(x == 1)
+    def _():
+        for h in range(2):
+            first_hop(h).wait_recv()
+            if nx == 4:
+                hop_out[h] = enter(whole_row[h], hop_in[h]).astype(bf16)
+                second_hop(h, True).start()
+                second_hop(h, False).start()
+
+    if nx == 4:
+        @pl.when(x == 2)
         def _():
-            hop(h).wait_recv()
-
-        @pl.when(x < nx - 1)
+            for h in range(2):
+                gam, mat = whole_row[h]
+                map_out[h, :W] = mat.astype(bf16)
+                hi = gam.astype(bf16).astype(f32)
+                mid = (gam - hi).astype(bf16).astype(f32)
+                low = gam - hi - mid
+                at = lax.broadcasted_iota(jnp.int32, (16, 2 * W), 0)
+                map_out[h, W:] = jnp.where(
+                    at == 0, hi, jnp.where(at == 1, mid, jnp.where(at == 2, low, 0.0))
+                ).astype(bf16)
+                map_hop(h).start()
+
+        @pl.when(x == 3)
         def _():
-            hop_out[h] = enter(whole_row[h], hop_in[h])
-            hop(h).start()
-
-    entering = [enter(prefix[h], hop_in[h]) for h in range(2)]
+            for h in range(2):
+                map_hop(h).wait_recv()
+                gam = jnp.sum(map_in[h, W:].astype(f32), axis=0, keepdims=True)[:, 0:1]
+                gam, mat = compose(prefix[h], (gam, map_in[h, :W].astype(f32)))
+                lead[h, :W] = mat
+                lead[h, W:] = jnp.broadcast_to(gam, (8, 2 * W))
+            for h in range(2):
+                second_hop(h, True).wait_recv()
+
+        @pl.when(x == 2)
+        def _():
+            for h in range(2):
+                second_hop(h, False).wait_recv()
+
+    @pl.when(x < 3)
+    def _():
+        for h in range(2):
+            lead[h, :W] = prefix[h][1]
+            lead[h, W:] = jnp.broadcast_to(prefix[h][0], (8, 2 * W))
+
+    entering = [
+        enter((lead[h, W : W + 1, 0:1], lead[h, :W]), hop_in[h]).astype(bf16) for h in range(2)
+    ]
 
     pieces = PIECES
     size = qeff_ref.shape[0] // pieces
@@ -384,7 +449,7 @@
         return dot(normed[0, p], weights[d, : 2 * W]) + dot(normed[1, p], weights[d, 2 * W :])
 
     def ring(s, p):
-        return remote(sent.at[s, p], came.at[s, p], ring_s.at[s, p], ring_r.at[s, p], target)
+        return remote(sent.at[s, p], came.at[s, p], ring_s.at[p], ring_r.at[s, p], target)
 
     def block_of(s):
         return lax.rem(y - step_y * (s + 1) + 2 * ny, ny)
@@ -398,10 +463,9 @@
         make_normed(p)
         normed_copy(p).start()
         if p == 0:
-            for d in range(ny):
-                own, far = weight_copies(d)
-                own.wait()
-                far.wait_recv()
+            own, far = all_weights()
+            own.wait()
+            far.wait_recv()
         if p > 0:
             first_step(p - 1)
     first_step(pieces - 1)
@@ -412,6 +476,7 @@
             mine = partial(p, d)
             ring(s - 1, p).wait_recv()
             sent[s, p] = (mine + came[s - 1, p].astype(f32)).astype(bf16)
+            ring(s - 1, p).wait_send()
             ring(s, p).start()
 
     loop(ny - 2, lambda s: step(s + 1))
@@ -423,23 +488,29 @@
     for t in range(half):
         for part in range(PARTS):
             for upward in ways(t, part):
-                around(t, part, upward).wait_send()
-    for dz in range(1, nz):
-        shrink_copy(dz).wait_send()
-    for d in range(ny):
-        weight_copies(d)[1].wait_send()
+                if t > 0 or part >= PARTS // 2:
+                    around(t, part, upward).wait_send()
+    all_shrinks().wait_send()
+    all_weights()[1].wait_send()
     for h in range(2):
-        @pl.when(x < nx - 1)
+        @pl.when(x == 0)
         def _():
-            hop(h).wait_send()
+            first_hop(h).wait_send()
+
+        if nx == 4:
+            @pl.when(x == 1)
+            def _():
+                second_hop(h, True).wait_send()
+                second_hop(h, False).wait_send()
+
+            @pl.when(x == 2)
+            def _():
+                map_hop(h).wait_send()
+
     for p in range(pieces):
         normed_copy(p).wait_send()
-
-    def drain(s):
-        for p in range(pieces):
-            ring(s, p).wait_send()
-
-    loop(ny - 1, drain)
+    for p in range(pieces):
+        ring(ny - 2, p).wait_send()
 
 
 def layer(sizes, *arrays):
@@ -473,17 +544,20 @@
             pltpu.VMEM((nz, 16, W), f32),
             pltpu.VMEM((2, W, W), bf16),
             pltpu.VMEM((2, W, W), bf16),
+            pltpu.VMEM((2, W + 16, 2 * W), bf16),
+            pltpu.VMEM((2, W + 16, 2 * W), bf16),
+            pltpu.VMEM((2, W + 8, 2 * W), f32),
             pltpu.VMEM((ny, 4 * W, W), bf16),
             pltpu.VMEM((2, PIECES, size, 2 * W), bf16),
             pltpu.VMEM((ny - 1, PIECES, size, W), bf16),
             pltpu.VMEM((ny - 1, PIECES, size, W), bf16),
             dma((8,)),
             dma((half, PARTS)), dma((half, PARTS)), dma((half, PARTS)), dma((half, PARTS)),
-            dma((nz,)), dma((nz,)),
-            dma((2,)), dma((2,)),
-            dma((ny,)), dma((ny,)), dma((ny,)),
+            dma(()), dma(()),
+            dma((8,)), dma((8,)),
+            dma(()), dma(()), dma(()),
             dma((PIECES,)), dma((PIECES,)),
-            dma((ny - 1, PIECES)), dma((ny - 1, PIECES)),
+            dma((PIECES,)), dma((ny - 1, PIECES)),
         ],
         compiler_params=pltpu.CompilerParams(
             collective_id=0, has_side_effects=True, vmem_limit_bytes=56 << 20

time: 76.4 us -> 74.4 us (0.974)
  Pallas kernels: 74.5 us -> 72.6 us
    pallas_call x1, Pallas kernels: 74.5 us -> 72.6 us  [layer(): pl.pallas_call(kernel, out_shape=jax.ShapeDtypeStruct((tokens, W), bf16),...]
where the time goes in v4:
time: 74.4 us; the launch traced here: 74.2 us
  Pallas kernels  72.6 us (98%)
  local copies, waits for them, and re-layouts  1.67 us (2%)
    pallas_call x1, Pallas kernels, layer(): pl.pallas_call(kernel, out_shape=jax.ShapeDtypeStruct((tokens, W), bf16),...  72.6 us
    unnamed x1, local copies, waits for them, and re-layouts  1.67 us

profile of v4, /device:TPU:6, one launch (start us, length us, event | category | flops | bytes accessed | tf_op | source)
XLA Modules:
  0.0 74.2 jit_solution(7027338739331328019)
XLA Ops:
  0.0 72.6 %shard_map.91 = bf16[1024,128]{1,0:T(8,128)(2,1)} custom-call(bf16[1024,128]{1,0:T(8,128)(2,1)} %refs_0_.1, bf16[1024,128]{1,0:T(8,128)(2,1)} %refs_1_.1, bf16[1024,256]{1,0:T(8,128)(2,1)} %refs_2_.1, bf16[1024,256]{1,0:T(8,128)(2,1)} %refs_3_.1, f32[2,1024]{1,0:T(2,128)} %refs_4_.1, f32[2,1024]{1,0:T(2,128)} %refs_5_.1, s32[8,128]{1,0:T(8,128)} %bitcast.2, ...), custom_call_target="tpu_custom_call" | custom-call | tf_op jit(solution)/shard_map/pallas_call | solution.py:527
  72.6 1.7 %copy.11 = bf16[1024,128]{1,0:T(8,128)(2,1)} copy(bf16[1024,128]{1,0:T(8,128)(2,1)} %shard_map.91) | data formatting | bytes 524288

commit v5 on v4

--- a/solution.py
+++ b/solution.py
@@ -161,7 +161,10 @@
         gam_ref[h, 0:1, :] = gams[h]
 
 
-def token_outputs(first, count, q_ref, k_ref, rows, cols, both_ref, maps_ref, gam_ref, qeff_ref, att_ref):
+def token_outputs(
+    first, count, q_ref, k_ref, rows, cols, both_ref, maps_ref, gam_ref, qeff_ref, att_ref,
+    gate_ref, gain_ref, open_ref,
+):
     scores = []
     for c in range(first, first + count):
         vec_r, vec_c = vectors_at(rows, cols, c)
@@ -186,12 +189,14 @@
             gam = gam_ref[h, 8 + c : 9 + c, :]
             qeff_ref[here, lanes] = (product[:, :W] + gam * reach).astype(bf16)
             att_ref[here, lanes] = product[:, W:] + mine[:, W:]
+            gate = gate_ref[here, lanes].astype(f32)
+            open_ref[here, lanes] = gain_ref[...] * (gate / (1.0 + jnp.exp(-gate)))
 
 
 def layer_kernel(
     sizes, q_hbm, k_hbm, v_hbm, gate_hbm, rate_hbm, log_hbm, start_hbm, gain_hbm, w_ref, out_ref,
     q_ref, k_ref, v_ref, gate_ref, rate_ref, log_ref, start_ref, gain_ref,
-    rows, cols, both_ref, maps_ref, total_ref, gam_ref, qeff_ref, att_ref,
+    rows, cols, both_ref, maps_ref, total_ref, gam_ref, qeff_ref, att_ref, open_ref,
     msg, got, shrinks, hop_out, hop_in, map_out, map_in, lead, weights, normed, sent, came,
     load, right_s, right_r, left_s, left_r, shrink_s, shrink_r, hop_s, hop_r,
     w_own, w_s, w_r, n_s, n_r, ring_s, ring_r,
@@ -225,7 +230,7 @@
         pl.semaphore_signal(barrier, inc=1, device_id=other, device_id_type=MESH)
 
     pairs = (
-        (log_hbm, log_ref), (rate_hbm, rate_ref), (start_hbm, start_ref), (k_hbm, k_ref), (q_hbm, q_ref),
+        (k_hbm, k_ref), (log_hbm, log_ref), (rate_hbm, rate_ref), (start_hbm, start_ref), (q_hbm, q_ref),
         (v_hbm, v_ref), (gate_hbm, gate_ref), (gain_hbm, gain_ref),
     )
     loads = [pltpu.make_async_copy(src, dst, load.at[n]) for n, (src, dst) in enumerate(pairs)]
@@ -264,7 +269,7 @@
         near, rest = weights.at[:, : 2 * W], weights.at[:, 2 * W :]
         return pltpu.make_async_copy(near, near, w_own), remote(rest, rest, w_s, w_r, sibling)
 
-    for n in range(5):
+    for n in range(4):
         loads[n].wait()
     gather_vectors(k_ref, rate_ref, log_ref, start_ref, rows, cols)
     total_ref[...] = jnp.zeros_like(total_ref)
@@ -275,7 +280,10 @@
         shard_maps(i, group, k_ref, v_ref, rows, cols, both_ref, maps_ref, total_ref, gam_ref)
 
     def outputs(first, count):
-        token_outputs(first, count, q_ref, k_ref, rows, cols, both_ref, maps_ref, gam_ref, qeff_ref, att_ref)
+        token_outputs(
+            first, count, q_ref, k_ref, rows, cols, both_ref, maps_ref, gam_ref, qeff_ref, att_ref,
+            gate_ref, gain_ref, open_ref,
+        )
 
     def pass_on(t, h):
         for upward in (True, False):
@@ -311,6 +319,8 @@
         own.start()
         far.start()
     shares = [chunks * n // half for n in range(half + 1)]
+    for n in (4, 6, 7):
+        loads[n].wait()
     outputs(0, shares[1])
     for part in range(PARTS // 2):
         for upward in ways(0, part):
@@ -429,9 +439,6 @@
 
     pieces = PIECES
     size = qeff_ref.shape[0] // pieces
-    for n in (6, 7):
-        loads[n].wait()
-    gain = gain_ref[...]
 
     def normed_copy(p):
         return remote(normed.at[0, p], normed.at[1, p], n_s.at[p], n_r.at[p], sibling)
@@ -442,8 +449,7 @@
             lanes = slice(h * W, (h + 1) * W)
             attended = att_ref[here, lanes] + dot(qeff_ref[here, lanes], entering[h])
             scale = lax.rsqrt(jnp.mean(attended * attended, axis=1, keepdims=True) + 1e-6)
-            gate = gate_ref[here, lanes].astype(f32)
-            normed[0, p, :, lanes] = (attended * scale * gain * (gate / (1.0 + jnp.exp(-gate)))).astype(bf16)
+            normed[0, p, :, lanes] = (attended * scale * open_ref[here, lanes]).astype(bf16)
 
     def partial(p, d):
         return dot(normed[0, p], weights[d, : 2 * W]) + dot(normed[1, p], weights[d, 2 * W :])
@@ -538,6 +544,7 @@
             pltpu.VMEM((2, W, 2 * W), f32),
             pltpu.VMEM((2, 8 + chunks, W), f32),
             pltpu.VMEM((tokens, 2 * W), bf16),
+            pltpu.VMEM((tokens, 2 * W), f32),
             pltpu.VMEM((tokens, 2 * W), f32),
             pltpu.VMEM((PARTS, PART_ROWS, 2 * W), bf16),
             pltpu.VMEM((nz, PARTS, PART_ROWS, 2 * W), bf16),
@@ -560,9 +567,9 @@
             dma((PIECES,)), dma((ny - 1, PIECES)),
         ],
         compiler_params=pltpu.CompilerParams(
-            collective_id=0, has_side_effects=True, vmem_limit_bytes=56 << 20
+            collective_id=0, has_side_effects=True, vmem_limit_bytes=48 << 20
         ),
-    )(*arrays)
+    )(*[pltpu.with_memory_space_constraint(a, pltpu.MemorySpace.HBM) for a in arrays])
 
 
 def build(mesh, sizes):

time: 74.4 us -> 72.5 us (0.974)
  local copies, waits for them, and re-layouts: 1.67 us -> 0.71 us
  Pallas kernels: 72.6 us -> 71.7 us
    unnamed x1, local copies, waits for them, and re-layouts: 1.67 us -> 0.71 us
    pallas_call x1, Pallas kernels: 72.6 us -> 71.7 us  [layer(): pl.pallas_call(kernel, out_shape=jax.ShapeDtypeStruct((tokens, W), bf16),...]
where the time goes in v5:
time: 72.5 us; the launch traced here: 72.4 us
  Pallas kernels  71.7 us (99%)
    pallas_call x1, Pallas kernels, layer(): pl.pallas_call(kernel, out_shape=jax.ShapeDtypeStruct((tokens, W), bf16),...  71.7 us

profile of v5, /device:TPU:6, one launch (start us, length us, event | category | flops | bytes accessed | tf_op | source)
XLA Modules:
  0.0 72.4 jit_solution(2916826810593053033)
XLA Ops:
  0.0 71.7 %shard_map.91 = bf16[1024,128]{1,0:T(8,128)(2,1)S(1)} custom-call(bf16[1024,128]{1,0:T(8,128)(2,1)} %refs_0_.1, bf16[1024,128]{1,0:T(8,128)(2,1)} %refs_1_.1, bf16[1024,256]{1,0:T(8,128)(2,1)} %refs_2_.1, bf16[1024,256]{1,0:T(8,128)(2,1)} %refs_3_.1, f32[2,1024]{1,0:T(2,128)} %refs_4_.1, f32[2,1024]{1,0:T(2,128)} %refs_5_.1, s32[8,128]{1,0:T(8,128)} %bitcast.2, ...), custom_call_target="tpu_custom_call" | custom-call | tf_op jit(solution)/shard_map/pallas_call | solution.py:533
  71.7 0.7 copy.11

commit v6 on v5

--- a/solution.py
+++ b/solution.py
@@ -8,7 +8,6 @@
 W = 128
 NX, NZ, NY = 4, 8, 8
 PIECES = 4
-GROUP = 4
 PARTS = 2
 PART_ROWS = 2 * W // PARTS
 f32, bf16 = jnp.float32, jnp.bfloat16
@@ -98,15 +97,14 @@
     return row, lax.rem(col, W)
 
 
-def shard_maps(i, group, k_ref, v_ref, rows, cols, both_ref, maps_ref, total_ref, gam_ref):
+def chunk_maps(chunks, k_ref, v_ref, rows, cols, both_ref):
     row, col = pair_iotas()
 
     def side(parts):
         return jnp.concatenate(parts, axis=1)
 
     found = []
-    for j in range(group):
-        c = group * i + j
+    for c in range(chunks):
         vec_r, vec_c = vectors_at(rows, cols, c)
         kc = chunk_at(k_ref, c)
         kk = dot_t(kc, kc) * vec_c[:, 5:6] * vec_r[5:6]
@@ -117,12 +115,11 @@
         for entry in found:
             entry[1] = refine(entry[1], entry[0], size)
     moves = {}
-    for j in range(group):
-        c = group * i + j
+    for c in range(chunks):
         vec_r, vec_c = vectors_at(rows, cols, c)
         kc = chunk_at(k_ref, c)
         k_turned = jnp.transpose(kc.astype(f32)).astype(bf16)
-        inverse = found[j][1]
+        inverse = found[c][1]
         rk_r = vec_r[5:6]
         reset_r, reset_c = vec_r[2:3], vec_c[:, 2:3]
         reset_last = reset_r[:, W - 1 : W]
@@ -139,26 +136,18 @@
             whole = jnp.where(reset_last == 0.0, jnp.exp(g_last), 0.0)
             both = side([erase[:, lanes], write[:, lanes]])
             both_ref[c, h] = both.astype(bf16)
-            moves[j, h] = (whole, dot(k_turned, (both * (tail_c * vec_c[:, 5:6])).astype(bf16)))
-    totals = [total_ref[h] for h in range(2)]
-    gams = [gam_ref[h, 0:1, :] for h in range(2)]
-    for j in range(group):
-        c = group * i + j
-        for h in range(2):
-            whole, moved = moves[j, h]
-            total, gam = totals[h], gams[h]
-            total_b = total.astype(bf16)
-            maps_ref[c, h] = total_b
-            gam_ref[h, pl.ds(8 + c, 1), :] = gam
-            totals[h] = (
-                whole * total
-                - dot(moved[:, :W].astype(bf16), total_b)
-                + jnp.concatenate([-gam * moved[:, :W], moved[:, W:]], axis=1)
-            )
-            gams[h] = gam * whole
-    for h in range(2):
-        total_ref[h] = totals[h]
-        gam_ref[h, 0:1, :] = gams[h]
+            moved = dot(k_turned, (both * (tail_c * vec_c[:, 5:6])).astype(bf16))
+            moves[c, h] = (whole, side([-moved[:, :W], moved[:, W:]]))
+    return moves
+
+
+def prefix_map(levels, count):
+    found = None
+    for depth in reversed(range(len(levels))):
+        if count >> depth & 1:
+            here = levels[depth][(count >> depth) - 1]
+            found = here if found is None else compose(here, found)
+    return found
 
 
 def token_outputs(
@@ -196,14 +185,13 @@
 def layer_kernel(
     sizes, q_hbm, k_hbm, v_hbm, gate_hbm, rate_hbm, log_hbm, start_hbm, gain_hbm, w_ref, out_ref,
     q_ref, k_ref, v_ref, gate_ref, rate_ref, log_ref, start_ref, gain_ref,
-    rows, cols, both_ref, maps_ref, total_ref, gam_ref, qeff_ref, att_ref, open_ref,
+    rows, cols, both_ref, maps_ref, gam_ref, qeff_ref, att_ref, open_ref,
     msg, got, shrinks, hop_out, hop_in, map_out, map_in, lead, weights, normed, sent, came,
     load, right_s, right_r, left_s, left_r, shrink_s, shrink_r, hop_s, hop_r,
     w_own, w_s, w_r, n_s, n_r, ring_s, ring_r,
 ):
     nx, nz, ny = sizes
     chunks = q_ref.shape[0] // W
-    group = min(GROUP, chunks)
     seq, head = lax.axis_index("seq"), lax.axis_index("head")
     x, z = seq // nz, lax.rem(seq, nz)
     y, core = head // 2, lax.rem(head, 2)
@@ -272,12 +260,7 @@
     for n in range(4):
         loads[n].wait()
     gather_vectors(k_ref, rate_ref, log_ref, start_ref, rows, cols)
-    total_ref[...] = jnp.zeros_like(total_ref)
-    gam_ref[...] = jnp.ones_like(gam_ref)
     loads[5].wait()
-
-    def work(i):
-        shard_maps(i, group, k_ref, v_ref, rows, cols, both_ref, maps_ref, total_ref, gam_ref)
 
     def outputs(first, count):
         token_outputs(
@@ -298,15 +281,20 @@
 
         lax.fori_loop(0, count, wrapped, 0)
 
-    if chunks == group:
-        work(0)
-    else:
-        loop(chunks // group, work)
+    moves = chunk_maps(chunks, k_ref, v_ref, rows, cols, both_ref)
+    trees = []
+    for h in range(2):
+        tree = [[moves[c, h] for c in range(chunks)]]
+        while len(tree[-1]) > 1:
+            last = tree[-1]
+            tree.append([compose(last[n + 1], last[n]) for n in range(0, len(last), 2)])
+        trees.append(tree)
+        gam_ref[h, 0:8, :] = jnp.broadcast_to(tree[-1][0][0], (8, W))
     pl.semaphore_wait(barrier, len(greeted))
     def send_own(h):
         for n in range(PARTS // 2):
             part = h * PARTS // 2 + n
-            msg[part] = total_ref[h, n * PART_ROWS : (n + 1) * PART_ROWS].astype(bf16)
+            msg[part] = trees[h][-1][0][1][n * PART_ROWS : (n + 1) * PART_ROWS].astype(bf16)
             for upward in (True, False):
                 around(0, part, upward).start()
 
@@ -321,6 +309,13 @@
     shares = [chunks * n // half for n in range(half + 1)]
     for n in (4, 6, 7):
         loads[n].wait()
+    for h in range(2):
+        maps_ref[0, h] = jnp.zeros((W, 2 * W), bf16)
+        gam_ref[h, 8:9, :] = jnp.ones((1, W), f32)
+        for c in range(1, chunks):
+            gam, mat = prefix_map(trees[h], c)
+            maps_ref[c, h] = mat.astype(bf16)
+            gam_ref[h, 8 + c : 9 + c, :] = jnp.broadcast_to(gam, (1, W))
     outputs(0, shares[1])
     for part in range(PARTS // 2):
         for upward in ways(0, part):
@@ -541,7 +536,6 @@
             pltpu.VMEM((chunks, W, 8), f32),
             pltpu.VMEM((chunks, 2, W, 2 * W), bf16),
             pltpu.VMEM((chunks, 2, W, 2 * W), bf16),
-            pltpu.VMEM((2, W, 2 * W), f32),
             pltpu.VMEM((2, 8 + chunks, W), f32),
             pltpu.VMEM((tokens, 2 * W), bf16),
             pltpu.VMEM((tokens, 2 * W), f32),

time: 72.5 us -> 71.9 us (level)
  no operation moved by 1% of the time
where the time goes in v6:
time: 71.9 us; the launch traced here: 71.8 us
  Pallas kernels  71 us (99%)
    pallas_call x1, Pallas kernels, layer(): pl.pallas_call(kernel, out_shape=jax.ShapeDtypeStruct((tokens, W), bf16),...  71 us

profile of v6, /device:TPU:6, one launch (start us, length us, event | category | flops | bytes accessed | tf_op | source)
XLA Modules:
  0.0 71.8 jit_solution(7286848466474994876)
XLA Ops:
  0.0 71.0 %shard_map.91 = bf16[1024,128]{1,0:T(8,128)(2,1)S(1)} custom-call(bf16[1024,128]{1,0:T(8,128)(2,1)} %refs_0_.1, bf16[1024,128]{1,0:T(8,128)(2,1)} %refs_1_.1, bf16[1024,256]{1,0:T(8,128)(2,1)} %refs_2_.1, bf16[1024,256]{1,0:T(8,128)(2,1)} %refs_3_.1, f32[2,1024]{1,0:T(2,128)} %refs_4_.1, f32[2,1024]{1,0:T(2,128)} %refs_5_.1, s32[8,128]{1,0:T(8,128)} %bitcast.2, ...), custom_call_target="tpu_custom_call" | custom-call | tf_op jit(solution)/shard_map/pallas_call | solution.py:528
  71.1 0.7 copy.11

commit v7 on v6

--- a/solution.py
+++ b/solution.py
@@ -312,10 +312,15 @@
     for h in range(2):
         maps_ref[0, h] = jnp.zeros((W, 2 * W), bf16)
         gam_ref[h, 8:9, :] = jnp.ones((1, W), f32)
-        for c in range(1, chunks):
-            gam, mat = prefix_map(trees[h], c)
-            maps_ref[c, h] = mat.astype(bf16)
-            gam_ref[h, 8 + c : 9 + c, :] = jnp.broadcast_to(gam, (1, W))
+
+    def prefixes(first, count):
+        for c in range(max(first, 1), first + count):
+            for h in range(2):
+                gam, mat = prefix_map(trees[h], c)
+                maps_ref[c, h] = mat.astype(bf16)
+                gam_ref[h, 8 + c : 9 + c, :] = jnp.broadcast_to(gam, (1, W))
+
+    prefixes(0, shares[1])
     outputs(0, shares[1])
     for part in range(PARTS // 2):
         for upward in ways(0, part):
@@ -327,6 +332,7 @@
         for part in range(PARTS):
             pass_on(t, part)
             if part == PARTS // 2 - 1:
+                prefixes(shares[t], shares[t + 1] - shares[t])
                 outputs(shares[t], shares[t + 1] - shares[t])
     for part in range(PARTS):
         for upward in ways(half - 1, part):

time: 71.9 us -> 71.9 us (level)
  no operation moved by 1% of the time
where the time goes in v7:
time: 71.9 us; the launch traced here: 71.8 us
  Pallas kernels  71.1 us (99%)
    pallas_call x1, Pallas kernels, layer(): pl.pallas_call(kernel, out_shape=jax.ShapeDtypeStruct((tokens, W), bf16),...  71.1 us

profile of v7, /device:TPU:6, one launch (start us, length us, event | category | flops | bytes accessed | tf_op | source)
XLA Modules:
  0.0 71.8 jit_solution(1092507827536946853)
XLA Ops:
  0.0 71.1 %shard_map.91 = bf16[1024,128]{1,0:T(8,128)(2,1)S(1)} custom-call(bf16[1024,128]{1,0:T(8,128)(2,1)} %refs_0_.1, bf16[1024,128]{1,0:T(8,128)(2,1)} %refs_1_.1, bf16[1024,256]{1,0:T(8,128)(2,1)} %refs_2_.1, bf16[1024,256]{1,0:T(8,128)(2,1)} %refs_3_.1, f32[2,1024]{1,0:T(2,128)} %refs_4_.1, f32[2,1024]{1,0:T(2,128)} %refs_5_.1, s32[8,128]{1,0:T(8,128)} %bitcast.2, ...), custom_call_target="tpu_custom_call" | custom-call | tf_op jit(solution)/shard_map/pallas_call | solution.py:534
  71.1 0.7 copy.11
